TPU v7x, 32 devices: a whole 2x2x4 slice. The times are simulated.
32 devices in a mesh: section: 2 (over y), fsdp: 4 (over x, core), replica: 4 (over z).
Axes of the slice: x: 2, y: 2, z: 4, core: 2. Of those that a mesh axis runs over, the one named last changes fastest.
Arguments:
- inputs: bfloat16 [2, 4, 512, 768], P(None, 'replica', 'fsdp'), may hold values from -6 to 6
- segments: int32 [2, 4, 512], P(None, 'replica'), may hold values from 0 to 4, as said below
- cotangent: bfloat16 [2, 4, 512, 768], P(None, 'replica', 'fsdp'), may hold values from -6 to 6
- ln1_gain: bfloat16 [2, 768], P('section', 'fsdp'), may hold values from 0.5 to 1.5
- ln1_bias: bfloat16 [2, 768], P('section', 'fsdp'), may hold values from -3 to 3
- qkv_weight: bfloat16 [2, 768, 2304], P('section', 'fsdp'), may hold values from -0.21875 to 0.21875
- qv_bias: bfloat16 [2, 1536], P('section', 'fsdp'), may hold values from -3 to 3
- out_weight: bfloat16 [2, 768, 768], P('section', 'fsdp'), may hold values from -0.875 to 0.875
- out_bias: bfloat16 [2, 768], P('section', 'fsdp'), may hold values from -3 to 3
- ln2_gain: bfloat16 [2, 768], P('section', 'fsdp'), may hold values from 0.5 to 1.5
- ln2_bias: bfloat16 [2, 768], P('section', 'fsdp'), may hold values from -3 to 3
- up_weight: bfloat16 [2, 768, 3072], P('section', 'fsdp'), may hold values from -0.21875 to 0.21875
- up_bias: bfloat16 [2, 3072], P('section', 'fsdp'), may hold values from -3 to 3
- down_weight: bfloat16 [2, 3072, 768], P('section', 'fsdp'), may hold values from -0.109375 to 0.109375
- down_bias: bfloat16 [2, 768], P('section', 'fsdp'), may hold values from -3 to 3
Outputs:
- acts: bfloat16 [2, 2, 4, 512, 768], P('section', None, 'replica', 'fsdp')
- grads_in: float32 [2, 2, 4, 512, 768], P('section', None, 'replica', 'fsdp')
- ln1_gain_grad: float32 [2, 768], P('section', 'fsdp')
- ln1_bias_grad: float32 [2, 768], P('section', 'fsdp')
- qkv_weight_grad: float32 [2, 768, 2304], P('section', 'fsdp')
- qv_bias_grad: float32 [2, 1536], P('section', 'fsdp')
- out_weight_grad: float32 [2, 768, 768], P('section', 'fsdp')
- out_bias_grad: float32 [2, 768], P('section', 'fsdp')
- ln2_gain_grad: float32 [2, 768], P('section', 'fsdp')
- ln2_bias_grad: float32 [2, 768], P('section', 'fsdp')
- up_weight_grad: float32 [2, 768, 3072], P('section', 'fsdp')
- up_bias_grad: float32 [2, 3072], P('section', 'fsdp')
- down_weight_grad: float32 [2, 3072, 768], P('section', 'fsdp')
- down_bias_grad: float32 [2, 768], P('section', 'fsdp')
Inputs may be any that keep to these rules, and one draw needn't show every extreme that they name: `segments`: along each sequence the numbers never fall and each of the five documents 0 to 4 is present; document 0 ends before position 128 and document 1 runs past position 384.
All inputs are finite; a program needn't handle non-finite values.
Results may differ from a plain program's by a relative error of at most 0.017.
Values may be sent and summed in bfloat16 or wider, within the bound.
No kernel may reach another device: no remote copies, remote signals or barrier semaphores. Data moves between devices by JAX's collectives and lax.ppermute only.
A program may use at most 192 MiB of HBM per device.

v0:
```python
import jax
import jax.numpy as jnp
from jax import lax
from jax.experimental import pallas as pl
from jax.experimental.pallas import tpu as pltpu
from jax.sharding import PartitionSpec as P

HEADS = 12
HD = 64
EPS = 1e-05
MASKED = -1e30
F32 = jnp.float32
BF16 = jnp.bfloat16
ROWS = 128


def across(value):
    return lax.ppermute(value, "fsdp", [(i, i ^ 2) for i in range(4)])


def between(value):
    return lax.ppermute(value, "fsdp", [(i, i ^ 1) for i in range(4)])


def ordered(place, own, other, axis=0):
    first = place == 0
    return jnp.stack([jnp.where(first, own, other), jnp.where(first, other, own)], axis)


def joined(place, own, other, axis=0):
    first = place == 0
    return jnp.concatenate([jnp.where(first, own, other), jnp.where(first, other, own)], axis)


def part_of(value, place, size, axis=0):
    return lax.dynamic_slice_in_dim(value, place * size, size, axis)


def pick(value, place, axis=0):
    return lax.dynamic_index_in_dim(value, place, axis, keepdims=False)


def matmul(left, right):
    return jnp.dot(left, right, preferred_element_type=F32)


def matmul_t(left, right):
    return lax.dot_general(left, right, (((1,), (1,)), ((), ())), preferred_element_type=F32)


def t_matmul(left, right):
    return lax.dot_general(left, right, (((0,), (0,)), ((), ())), preferred_element_type=F32)


def normalised(values):
    centred = values - jnp.mean(values, axis=-1, keepdims=True)
    inverse = lax.rsqrt(jnp.mean(centred * centred, axis=-1, keepdims=True) + EPS)
    return centred * inverse, inverse


def norm_back(grad, xhat, inverse, gain):
    scaled = grad * gain
    return inverse * (
        scaled
        - jnp.mean(scaled, axis=-1, keepdims=True)
        - xhat * jnp.mean(scaled * xhat, axis=-1, keepdims=True)
    )


def gelu_parts(u):
    a = 0.7978845608028654
    b = 0.044715
    t = jnp.tanh(a * (u + b * u * u * u))
    value = 0.5 * u * (1.0 + t)
    slope = 0.5 * (1.0 + t) + 0.5 * u * (1.0 - t * t) * a * (1.0 + 3.0 * b * u * u)
    return value, slope


def feed(middle, w):
    xhat, inverse = normalised(middle)
    normed = (xhat * w["ln2_gain"] + w["ln2_bias"]).astype(BF16)
    activated, slopes = [], []
    part = None
    for up, bias, down in zip(w["up"], w["up_bias"], w["down"]):
        value, slope = gelu_parts(matmul(normed, up) + bias)
        value, slope = lax.optimization_barrier((value.astype(BF16), slope.astype(BF16)))
        activated.append(value)
        slopes.append(slope)
        term = matmul(value, down)
        part = term if part is None else part + term
    return part, (normed, activated, slopes)


def forward(hidden, attention, w, core):
    part, *attn_state = attention(hidden)
    middle = hidden.astype(F32) + part.astype(F32) + between(part).astype(F32) + w["out_bias"]
    part, feed_state = feed(middle, w)
    rows = part.shape[0] // 2
    other = between(part_of(part, 1 - core, rows).astype(BF16))
    result = part_of(middle, core, rows) + part_of(part, core, rows) + other.astype(F32) + w["down_bias"]
    return result.astype(BF16), (middle, attn_state, feed_state)


def feed_back(grad, slopes, w):
    g_pre = []
    part = None
    for slope, up, down in zip(slopes, w["up"], w["down"]):
        g = (matmul_t(grad, down) * slope.astype(F32)).astype(BF16)
        g_pre.append(g)
        term = matmul_t(g, up)
        part = term if part is None else part + term
    return g_pre, part.astype(BF16)


def call(kernel, outs, scratch, args, flops, smem=()):
    spec = pl.BlockSpec(memory_space=pltpu.VMEM)
    moved = sum(a.size * a.dtype.itemsize for a in args)
    moved += sum(o.size * o.dtype.itemsize for o in outs)
    return pl.pallas_call(
        kernel,
        out_shape=tuple(outs),
        in_specs=[pl.BlockSpec(memory_space=pltpu.SMEM) if i in smem else spec for i in range(len(args))],
        out_specs=tuple(spec for _ in outs),
        scratch_shapes=scratch,
        compiler_params=pltpu.CompilerParams(vmem_limit_bytes=40 << 20),
        cost_estimate=pl.CostEstimate(flops=flops, bytes_accessed=moved, transcendentals=0),
    )(*args)


def shape(dims, kind):
    return jax.ShapeDtypeStruct(dims, kind)


def split_heads(pair):
    lane = lax.broadcasted_iota(jnp.int32, pair.shape, 1)
    zero = jnp.zeros_like(pair)
    return jnp.concatenate([jnp.where(lane < HD, pair, zero), jnp.where(lane < HD, zero, pair)], axis=0)


def join_heads(stacked):
    rows = stacked.shape[0] // 2
    lane = lax.broadcasted_iota(jnp.int32, (rows, stacked.shape[1]), 1)
    return jnp.where(lane < HD, stacked[:rows], stacked[rows:])


def attend_kernel(
    hidden, seg_col, seg_row, gain, offset, w_qkv, bias, w_out, part, normed, qkv, mixed, probs
):
    rows, width = hidden.shape
    half = w_qkv.shape[1] // 3

    @pl.loop(0, rows // ROWS)
    def _(i):
        at = pl.ds(pl.multiple_of(i * ROWS, ROWS), ROWS)
        xhat, _ = normalised(hidden[at, :].astype(F32))
        normed[at, :] = (xhat * gain[...] + offset[...]).astype(BF16)

    @pl.loop(0, 3)
    def _(i):
        at = pl.ds(pl.multiple_of(i * half, half), half)
        qkv[:, at] = (matmul(normed[...], w_qkv[:, at]) + bias[:, at]).astype(BF16)

    for i in range(rows // ROWS):
        at = slice(i * ROWS, (i + 1) * ROWS)
        seen = (i + 1) * ROWS
        query_at = i * ROWS + lax.broadcasted_iota(jnp.int32, (ROWS, seen), 0)
        key_at = lax.broadcasted_iota(jnp.int32, (ROWS, seen), 1)
        allowed = (key_at <= query_at) & (seg_col[at, :] == seg_row[:, :seen])
        penalty = jnp.where(allowed, 0.0, MASKED)
        penalty = jnp.concatenate([penalty, penalty], axis=0)
        for j in range(half // 128):
            q = split_heads(qkv[at, j * 128 : (j + 1) * 128] * jnp.bfloat16(HD**-0.5))
            k = qkv[:seen, half + j * 128 : half + (j + 1) * 128]
            v = qkv[:seen, 2 * half + j * 128 : 2 * half + (j + 1) * 128]
            scores = jnp.where(penalty == 0.0, matmul_t(q, k), MASKED)
            exps = jnp.exp(scores - jnp.max(scores, axis=-1, keepdims=True))
            p = (exps * (1.0 / jnp.sum(exps, axis=-1, keepdims=True))).astype(BF16)
            probs[j, i, :, :seen] = p
            mixed[at, j * 128 : (j + 1) * 128] = join_heads(matmul(p, v)).astype(BF16)

    @pl.loop(0, 2)
    def _(i):
        at = pl.ds(pl.multiple_of(i * 256, 256), 256)
        part[at, :] = matmul(mixed[at, :], w_out[...]).astype(BF16)


def attend(hidden, seg_col, seg_row, w):
    rows, width = hidden.shape
    half = w["qkv"].shape[1] // 3
    args = [hidden, seg_col, seg_row, w["ln1_gain"][None], w["ln1_bias"][None], w["qkv"], w["qkv_bias"][None], w["out"]]
    outs = [shape((rows, width), BF16)]
    kept = [shape((rows, width), BF16), shape((rows, 3 * half), BF16), shape((rows, half), BF16)]
    outs += kept + [shape((half // 128, rows // ROWS, 2 * ROWS, rows), BF16)]
    flops = 2 * rows * (width * 4 * half + 4 * rows * half)
    return call(attend_kernel, outs, [], args, flops)


def attend_back_kernel(
    own, other, grad, middle, gain, w_out, qkv, probs, w_qkv,
    g_middle, g_branch, g_qkv, part, sums, g_mixed, g_key, g_value
):
    rows, width = grad.shape
    half = w_qkv.shape[1] // 3
    scale = HD**-0.5
    sums[...] = jnp.zeros_like(sums)

    @pl.loop(0, rows // ROWS)
    def _(i):
        at = pl.ds(pl.multiple_of(i * ROWS, ROWS), ROWS)
        g_norm = own[at, :].astype(F32) + other[at, :].astype(F32)
        xhat, inverse = normalised(middle[at, :])
        value = grad[at, :].astype(F32) + norm_back(g_norm, xhat, inverse, gain[...])
        g_middle[at, :] = value
        branch = value.astype(BF16)
        g_branch[at, :] = branch
        sums[0:1, :] += jnp.sum(g_norm * xhat, axis=0, keepdims=True)
        sums[1:2, :] += jnp.sum(g_norm, axis=0, keepdims=True)
        sums[2:3, :] += jnp.sum(branch.astype(F32), axis=0, keepdims=True)

    g_mixed[...] = matmul_t(g_branch[...], w_out[...]).astype(BF16)

    for i in reversed(range(rows // ROWS)):
        at = slice(i * ROWS, (i + 1) * ROWS)
        seen = (i + 1) * ROWS
        for j in range(half // 128):
            lanes = slice(j * 128, (j + 1) * 128)
            q = split_heads(qkv[at, lanes] * jnp.bfloat16(scale))
            k = qkv[:seen, half + j * 128 : half + (j + 1) * 128] * jnp.bfloat16(scale)
            v = qkv[:seen, 2 * half + j * 128 : 2 * half + (j + 1) * 128]
            g = split_heads(g_mixed[at, lanes])
            p = probs[j, i, :, :seen]
            p_full = p.astype(F32)
            g_probs = matmul_t(g, v)
            inner = jnp.sum(p_full * g_probs, axis=-1, keepdims=True)
            g_scores = (p_full * (g_probs - inner)).astype(BF16)
            g_qkv[at, lanes] = join_heads(matmul(g_scores, k)).astype(BF16)
            key_term = t_matmul(g_scores, q)
            value_term = t_matmul(p, g)
            if seen == rows:
                g_key[:, lanes] = key_term
                g_value[:, lanes] = value_term
            else:
                g_key[:seen, lanes] += key_term
                g_value[:seen, lanes] += value_term
    g_qkv[:, half : 2 * half] = g_key[...].astype(BF16)
    g_qkv[:, 2 * half :] = g_value[...].astype(BF16)

    @pl.loop(0, 2)
    def _(i):
        at = pl.ds(pl.multiple_of(i * 256, 256), 256)
        part[at, :] = matmul_t(g_qkv[at, :], w_qkv[...]).astype(BF16)


def attend_back(own, other, grad, middle, qkv, probs, w):
    rows, width = grad.shape
    half = w["qkv"].shape[1] // 3
    args = [own, other, grad, middle, w["ln2_gain"][None], w["out"], qkv, probs, w["qkv"]]
    outs = [
        shape((rows, width), F32),
        shape((rows, width), BF16),
        shape((rows, 3 * half), BF16),
        shape((rows, width), BF16),
        shape((8, width), F32),
    ]
    scratch = [
        pltpu.VMEM((rows, half), BF16),
        pltpu.VMEM((rows, half), F32),
        pltpu.VMEM((rows, half), F32),
    ]
    flops = 2 * rows * (width * 4 * half + 8 * rows * half)
    return call(attend_back_kernel, outs, scratch, args, flops)


def feed_back_kernel(grad, *refs):
    slopes, ups, downs, (part,) = refs[0:2], refs[2:4], refs[4:6], refs[6:]
    half = grad.shape[0] // 2

    @pl.loop(0, 2)
    def _(i):
        at = pl.ds(pl.multiple_of(i * half, half), half)
        total = None
        for slope, up, down in zip(slopes, ups, downs):
            g = (matmul_t(grad[at, :], down[...]) * slope[at, :].astype(F32)).astype(BF16)
            term = matmul_t(g, up[...])
            total = term if total is None else total + term
        part[at, :] = total.astype(BF16)


def feed_back_rows(grad, slopes, w):
    args = [grad, *slopes, *w["up"], *w["down"]]
    flops = 8 * grad.size * w["up"][0].shape[1]
    return call(feed_back_kernel, [shape(grad.shape, BF16)], [], args, flops)[0]


def input_back(part, hidden, g_middle, w, core):
    rows = part.shape[0] // 2
    g_norm1 = part_of(part, core, rows).astype(F32) + between(part_of(part, 1 - core, rows)).astype(F32)
    xhat1, inv1 = normalised(part_of(hidden, core, rows).astype(F32))
    own_middle = part_of(g_middle, core, rows)
    return own_middle + norm_back(g_norm1, xhat1, inv1, w["ln1_gain"]), g_norm1, xhat1


def tied(value, *others):
    return lax.optimization_barrier((value,) + others)[0]


class Sums:
    HOPS = ([(0, 1), (3, 2)], [(1, 2), (2, 1)], [(1, 0), (2, 3)])

    def __init__(self, count):
        self.line = lax.axis_size("replica") == 4
        place = lax.axis_index("replica")
        self.outer = (place == 0) | (place == 3)
        self.values = {}
        self.results = {}
        self.last = None
        stages = 4 if self.line else 1
        self.events = sorted((p + s, -s, p) for p in range(count) for s in range(stages))

    def chained(self, value):
        if self.last is not None:
            value = tied(value, self.last)
        self.last = value
        return value

    def put(self, piece, sides, after):
        sides = [(mine, across(other.astype(BF16))) for mine, other in sides]
        self.values[piece] = (sides, after)

    def run(self, until=None):
        while self.events:
            _, stage, piece = self.events.pop(0)
            stage = -stage
            if stage == 0:
                sides, after = self.values[piece]
                totals = [mine.astype(F32) + self.chained(got).astype(F32) for mine, got in sides]
                totals = [total.astype(BF16) for total in totals]
                seen = totals[0]
                value = after(*totals)
                if not self.line:
                    self.results[piece] = lax.psum(value.astype(F32), "replica")
            else:
                value, got = self.values[piece]
                got = self.chained(got)
                if stage == 3:
                    self.results[piece] = jnp.where(self.outer, got, value).astype(F32)
                else:
                    value = (value.astype(F32) + got.astype(F32)).astype(BF16)
                seen = value
            if self.line and stage < 3:
                self.values[piece] = (value, lax.ppermute(value, "replica", self.HOPS[stage]))
            if until == (piece, stage):
                break
        return seen


def shards(
    inputs,
    segments,
    cotangent,
    ln1_gain,
    ln1_bias,
    qkv_weight,
    qv_bias,
    out_weight,
    out_bias,
    ln2_gain,
    ln2_bias,
    up_weight,
    up_bias,
    down_weight,
    down_bias,
):
    place = lax.axis_index("fsdp")
    chip, core = place // 2, place % 2
    is_first = lax.axis_index("section") == 0
    width = inputs.shape[-1]
    half = width // 2
    shard = width // 4
    hidden_units = up_weight.shape[-1]
    group = hidden_units // 4

    def both(rows):
        return joined(core, rows, between(rows))

    def entered(values):
        mine = pick(values, chip, 0)[0]
        other = across(pick(values, 1 - chip, 0)[0])
        pair = ordered(chip, mine, other)
        return ordered(core, pair, between(pair), 1).reshape(-1, width), other

    small = jnp.concatenate(
        [v[0] for v in (ln1_gain, ln1_bias, qv_bias, out_bias, ln2_gain, ln2_bias, up_bias, down_bias)]
    )
    pair = ordered(core, small, between(small))
    small = ordered(chip, pair, across(pair)).reshape(4, -1).astype(F32)
    sizes = [shard, shard, 2 * shard, shard, shard, shard, group, shard]
    vectors = []
    at = 0
    for size in sizes:
        vectors.append(small[:, at : at + size].reshape(-1))
        at += size
    hidden, first = entered(inputs)

    def rows_of(value, size):
        count = value.shape[1] // (2 * size)
        sides = [
            jnp.concatenate([part_of(value, 2 * i + place, size, 1) for i in range(count)], 1)
            for place in (core, 1 - core)
        ]
        return joined(core, sides[0], between(sides[1]))

    own_qkv = rows_of(qkv_weight[0], half)
    got_qkv = across(qkv_weight[0])
    qkv = joined(chip, own_qkv, rows_of(got_qkv, half))

    got_out = tied(across(tied(out_weight[0], first)), got_qkv)
    same = chip == core
    out = joined(
        core,
        jnp.where(same, out_weight[0], got_out),
        between(jnp.where(same, got_out, out_weight[0])),
    )

    own, other = (part_of(up_weight[0], place, 2 * group, 1) for place in (chip, 1 - chip))
    got_up = tied(across(tied(other, first)), got_out)
    got_other = tied(across(tied(own, got_qkv)), got_up)
    got_down = tied(across(tied(down_weight[0][: group // 2], got_out)), got_other)
    got_last = tied(across(tied(down_weight[0][group // 2 :], got_up)), got_down)
    own, other = rows_of(own, group), rows_of(other, group)
    up = [
        joined(chip, own, rows_of(got_up, group)),
        joined(chip, other, rows_of(got_other, group)),
    ]
    down = [down_weight[0], jnp.concatenate([got_down, got_last])]

    qv = vectors[2].reshape(2, 2, half)
    zeros = jnp.zeros((half,), F32)
    up_vector = pick(vectors[6].reshape(2, 2, group), core, 1)
    w = {
        "ln1_gain": vectors[0],
        "ln1_bias": vectors[1],
        "qkv": qkv,
        "qkv_bias": jnp.concatenate([pick(qv[0], core), zeros, pick(qv[1], core)]),
        "out": out,
        "out_bias": vectors[3],
        "ln2_gain": vectors[4],
        "ln2_bias": vectors[5],
        "up": up,
        "up_bias": [pick(up_vector, chip), pick(up_vector, 1 - chip)],
        "down": down,
        "down_bias": vectors[7],
    }
    segment = pick(segments, chip, 0)[0]

    def attention(rows):
        return attend(rows, segment[:, None], segment[None], w)

    result, _ = forward(hidden, attention, w, core)
    arrived = both(lax.ppermute(result, "section", [(0, 1)]))
    grad, _ = entered(tied(cotangent, result))
    hidden = jnp.where(is_first, hidden, arrived)
    result, state = forward(hidden, attention, w, core)
    middle, attn_state, (normed2, activated, slopes) = state
    normed1, qkv_rows, mixed, probs = attn_state

    part = feed_back_rows(grad, slopes, w)
    g_middle, _, _, part, _ = attend_back(part, between(part), grad, middle, qkv_rows, probs, w)
    g_input, _, _ = input_back(part, hidden, g_middle, w, core)

    def left(value):
        block = value.shape[0] // 2
        pair = ordered(core, part_of(value, core, block), between(part_of(value, 1 - core, block)))
        return ordered(chip, pick(pair, chip), across(pick(pair, 1 - chip)))[None, :, None]

    arrived = both(lax.ppermute(g_input.astype(BF16), "section", [(1, 0)]))
    acts = left(tied(result, g_input))
    grad = jnp.where(is_first, arrived, grad)

    sums = Sums(4)
    rows = hidden.shape[0]

    def sides(values):
        return tuple(part_of(values, place, half, 1) for place in (chip, 1 - chip))

    def swapped(value):
        return jnp.concatenate([part_of(value, core, shard), between(part_of(value, 1 - core, shard))])

    other = t_matmul(activated[1], grad).astype(BF16)
    sums.put(0, [(t_matmul(activated[0], grad), other)], lambda v: v)
    g_pre, part = feed_back(grad, slopes, w)
    stay, leave = sides(normed2)
    up_sides = [(t_matmul(stay, g_pre[i]), t_matmul(leave, g_pre[1 - i])) for i in range(2)]
    sums.put(1, up_sides, lambda a, b: jnp.concatenate([swapped(a), swapped(b)]))
    other = between(part)
    g_middle, g_branch, g_qkv, part, norm_sums = attend_back(part, other, grad, middle, qkv_rows, probs, w)

    stay, leave = (t_matmul(side, g_qkv) for side in sides(normed1))
    term = t_matmul(mixed, g_branch).astype(BF16)
    term = joined(core, part_of(term, core, shard), between(part_of(term, 1 - core, shard)))

    def folded(value):
        return jnp.concatenate([value[:, :half], value[:, half:]])

    sums.put(2, [(stay[:, :width], leave[:, :width])], swapped)
    stay = jnp.concatenate([stay[:, width:], folded(part_of(term, chip, shard)).astype(F32)], 1)
    leave = jnp.concatenate([leave[:, width:].astype(BF16), folded(part_of(term, 1 - chip, shard))], 1)
    part = tied(part, leave, sums.run((0, 0)))
    g_input, g_norm1, xhat1 = input_back(part, hidden, g_middle, w, core)

    def once(value):
        return jnp.where(core == 0, value, 0.0)

    def placed_half(value):
        return ordered(core, value, jnp.zeros_like(value))

    ones = jnp.ones((8, rows), BF16)

    def column_sums(values):
        return matmul(ones, values)[0]

    bias_sums = column_sums(g_qkv).reshape(3, half)
    qv_grad = jnp.concatenate([placed_half(bias_sums[0]), placed_half(bias_sums[2])])
    up_sums = ordered(chip, *(column_sums(g) for g in g_pre))
    up_bias_grad = ordered(core, up_sums, jnp.zeros_like(up_sums), 1)
    small_grads = [
        jnp.sum(g_norm1 * xhat1, axis=0),
        jnp.sum(g_norm1, axis=0),
        qv_grad,
        once(norm_sums[2]),
        once(norm_sums[0]),
        once(norm_sums[1]),
        up_bias_grad,
        once(column_sums(grad)),
    ]
    small_grads = jnp.concatenate([v.reshape(2, 2, -1) for v in small_grads], axis=-1)
    small_grads = pick(small_grads, core, 1) + between(pick(small_grads, 1 - core, 1))
    small_grads = small_grads.reshape(2, 3, width)
    def last_piece(value, vectors):
        return jnp.concatenate([jnp.concatenate([swapped(value[:, :half]), value[:, half:]], 1), vectors])

    sums.put(3, [(stay, leave), (pick(small_grads, chip), pick(small_grads, 1 - chip))], last_piece)
    grads_in = left(g_input.astype(BF16)).astype(F32)
    sums.run()
    done = sums.results
    down_grad = done[0]
    units = jnp.split(done[1], 4)
    up_grad = joined(chip, *(joined(core, units[2 * i], units[2 * i + 1], 1) for i in range(2)), 1)
    query_key, value_out, small_grads = done[2], done[3][: 2 * shard], done[3][2 * shard :].reshape(-1)
    qkv_grad = [
        joined(core, u[:shard], u[shard:], 1)
        for u in (query_key[:, :half], query_key[:, half:], value_out[:, :half])
    ]
    qkv_grad = jnp.concatenate(qkv_grad, 1)
    out_grad = jnp.concatenate([value_out[:shard, half:], value_out[shard:, half:]], 1)
    small_out = []
    at = 0
    for size in sizes:
        small_out.append(small_grads[None, at : at + size])
        at += size
    g_ln1g, g_ln1b, g_qv, g_outb, g_ln2g, g_ln2b, g_upb, g_downb = small_out
    return (
        acts,
        grads_in,
        g_ln1g,
        g_ln1b,
        qkv_grad[None],
        g_qv,
        out_grad[None],
        g_outb,
        g_ln2g,
        g_ln2b,
        up_grad[None],
        g_upb,
        down_grad[None],
        g_downb,
    )


def solution(mesh):
    rows = P(None, "replica", "fsdp", None)
    vector = P("section", "fsdp")
    matrix = P("section", "fsdp", None)
    layer = P("section", None, "replica", "fsdp", None)
    weights = (
        vector,
        vector,
        matrix,
        vector,
        matrix,
        vector,
        vector,
        vector,
        matrix,
        vector,
        matrix,
        vector,
    )
    return jax.shard_map(
        shards,
        mesh=mesh,
        in_specs=(rows, P(None, "replica", None), rows) + weights,
        out_specs=(layer, layer) + weights,
        check_vma=False,
    )
```

profile of v0, /device:TPU:0, one launch (start us, length us, event | category | flops | bytes accessed | tf_op | source)
XLA Modules:
  0.0 398.7 jit_solution(11314957785297200110)
XLA Ops:
  8.5 2.5 collective-permute-start
  11.1 2.1 dynamic-slice_bitcast_fusion.11
  20.1 15.9 %collective-permute-done.3 = bf16[2,2304]{1,0:T(2,128)(2,1)S(1)} collective-permute-done((bf16[2,2304]{1,0:T(2,128)(2,1)S(1)}, bf16[2,2304]{1,0:T(2,128)(2,1)S(1)}, u32[]{:S(2)}, u32[]{:S(2)}) %collective-permute-start.3) | collective-permute-done | bytes 9248 | tf_op jit(solution)/shard_map/ppermute | solution.py:18
  43.5 5.0 %collective-permute-done.7 = bf16[192,768]{1,0:T(8,128)(2,1)S(1)} collective-permute-done((bf16[192,768]{1,0:T(8,128)(2,1)S(1)}, bf16[192,768]{1,0:T(8,128)(2,1)S(1)}, u32[]{:S(2)}, u32[]{:S(2)}) %collective-permute-start.7) | collective-permute-done | bytes 294944 | tf_op jit(solution)/shard_map/ppermute | solution.py:18
  52.3 8.8 %collective-permute-done.11 = bf16[192,1536]{1,0:T(8,128)(2,1)S(1)} collective-permute-done((bf16[192,1536]{1,0:T(8,128)(2,1)}, bf16[192,1536]{1,0:T(8,128)(2,1)S(1)}, u32[]{:S(2)}, u32[]{:S(2)}) %collective-permute-start.11) | collective-permute-done | bytes 589856 | tf_op jit(solution)/shard_map/ppermute | solution.py:18
  64.1 9.7 %collective-permute-done.14 = bf16[192,1536]{1,0:T(8,128)(2,1)S(1)} collective-permute-done((bf16[192,1536]{1,0:T(8,128)(2,1)S(1)}, bf16[192,1536]{1,0:T(8,128)(2,1)S(1)}, u32[]{:S(2)}, u32[]{:S(2)}) %collective-permute-start.14) | collective-permute-done | bytes 589856 | tf_op jit(solution)/shard_map/ppermute | solution.py:18
  73.8 9.8 %shard_map.254 = (bf16[512,768]{1,0:T(8,128)(2,1)S(1)}, bf16[512,768]{1,0:T(8,128)(2,1)}, bf16[512,1152]{1,0:T(8,128)(2,1)}, bf16[512,384]{1,0:T(8,128)(2,1)}, bf16[3,4,256,512]{3,2,1,0:T(8,128)(2,1)}) custom-call(bf16[512,768]{1,0:T(8,128)(2,1)S(1)} %bitcast.191, s32[512,1]{1,0:T(8,128)S(1)} %copy.38.seg_col, s32[1,512]{1,0:T(1,128)S(1)} %get-tuple-element.256.seg_row, ...), custom_call_target="tpu_custom_call" | custom-call | flops 2013265920 | bytes 9452032 | tf_op jit(solution)/shard_map/pallas_call | solution.py:119
  84.1 2.2 collective-permute-done.16
  86.4 11.8 %collective-permute-done.17 = bf16[384,768]{1,0:T(8,128)(2,1)S(1)} collective-permute-done((bf16[384,768]{1,0:T(8,128)(2,1)S(1)}, bf16[384,768]{1,0:T(8,128)(2,1)S(1)}, u32[]{:S(2)}, u32[]{:S(2)}) %collective-permute-start.17) | collective-permute-done | bytes 589856 | tf_op jit(solution)/shard_map/ppermute | solution.py:18
  108.1 2.4 add_convert_fusion.15
  110.5 4.4 %collective-permute-start.19 = (bf16[256,768]{1,0:T(8,128)(2,1)}, bf16[256,768]{1,0:T(8,128)(2,1)}, u32[]{:S(2)}, u32[]{:S(2)}) collective-permute-start(bf16[256,768]{1,0:T(8,128)(2,1)} %add_convert_fusion.15), channel_id=1, source_target_pairs={{0,16},{1,17},{2,18},{3,19},{4,20},{5,21},{6,22},{7,23},{8,24},{9,... | collective-permute-start | bytes 1179656 | tf_op jit(solution)/shard_map/ppermute | solution.py:460
  119.5 3.6 collective-permute-done.19
  128.4 7.3 %shard_map.255 = (bf16[512,768]{1,0:T(8,128)(2,1)S(1)}, bf16[512,768]{1,0:T(8,128)(2,1)S(1)}, bf16[512,1152]{1,0:T(8,128)(2,1)S(1)}, bf16[512,384]{1,0:T(8,128)(2,1)S(1)}, bf16[3,4,256,512]{3,2,1,0:T(8,128)(2,1)S(1)}) custom-call(bf16[512,768]{1,0:T(8,128)(2,1)S(1)} %maximum_select_fusion.hidden, s32[512,1]{1,0:T(8,128)S(1)} %copy-done.22, ...), custom_call_target="tpu_custom_call" | custom-call | flops 2013265920 | bytes 9452032 | tf_op jit(solution)/shard_map/pallas_call | solution.py:119
  145.3 3.5 shard_map.256.own
  151.2 12.0 %shard_map.257 = (f32[512,768]{1,0:T(8,128)S(1)}, bf16[512,768]{1,0:T(8,128)(2,1)}, bf16[512,1152]{1,0:T(8,128)(2,1)}, bf16[512,768]{1,0:T(8,128)(2,1)S(1)}, f32[8,768]{1,0:T(8,128)}) custom-call(bf16[512,768]{1,0:T(8,128)(2,1)S(1)} %shard_map.256.own, bf16[512,768]{1,0:T(8,128)(2,1)S(1)} %collective-permute-done.25.other, bf16[512,768]{1,0:T(8,128)(2,1)S(1)} %bitcast.193, ...), custom_call_target="tpu_custom_call" | custom-call | flops 2818572288 | bytes 14969856 | tf_op jit(solution)/shard_map/pallas_call | solution.py:119
  173.0 8.0 %collective-permute-done.29 = bf16[256,768]{1,0:T(8,128)(2,1)} collective-permute-done((bf16[256,768]{1,0:T(8,128)(2,1)}, bf16[256,768]{1,0:T(8,128)(2,1)}, u32[]{:S(2)}, u32[]{:S(2)}) %collective-permute-start.29) | collective-permute-done | bytes 393248 | tf_op jit(solution)/shard_map/ppermute | solution.py:476
  196.4 2.7 convolution_convert_fusion.2
  199.6 2.6 convolution_convert_fusion.3
  206.8 11.4 %shard_map.258 = (f32[512,768]{1,0:T(8,128)S(1)}, bf16[512,768]{1,0:T(8,128)(2,1)S(1)}, bf16[512,1152]{1,0:T(8,128)(2,1)S(1)}, bf16[512,768]{1,0:T(8,128)(2,1)S(1)}, f32[8,768]{1,0:T(8,128)S(1)}) custom-call(bf16[512,768]{1,0:T(8,128)(2,1)S(1)} %copy-done.18, bf16[512,768]{1,0:T(8,128)(2,1)} %collective-permute-done.31.other, ...), custom_call_target="tpu_custom_call" | custom-call | flops 2818572288 | bytes 14969856 | tf_op jit(solution)/shard_map/pallas_call | solution.py:119
  224.1 3.2 add_convert_fusion.4
  227.3 4.5 %collective-permute-start.40 = (bf16[768,768]{1,0:T(8,128)(2,1)}, bf16[768,768]{1,0:T(8,128)(2,1)}, u32[]{:S(2)}, u32[]{:S(2)}) collective-permute-start(bf16[768,768]{1,0:T(8,128)(2,1)} %add_convert_fusion.4), channel_id=1, source_target_pairs={{0,1},{3,2},{4,5},{7,6},{8,9},{11,10},{12,13},{15,14},{16,17},{19,... | collective-permute-start | bytes 3538952 | tf_op jit(solution)/shard_map/ppermute | solution.py:351
  239.5 16.6 %collective-permute-done.40 = bf16[768,768]{1,0:T(8,128)(2,1)} collective-permute-done((bf16[768,768]{1,0:T(8,128)(2,1)}, bf16[768,768]{1,0:T(8,128)(2,1)}, u32[]{:S(2)}, u32[]{:S(2)}) %collective-permute-start.40) | collective-permute-done | bytes 1179680 | tf_op jit(solution)/shard_map/ppermute | solution.py:351
  260.4 2.9 add_convert_fusion.3
  266.4 7.3 %collective-permute-start.44 = (bf16[768,768]{1,0:T(8,128)(2,1)}, bf16[768,768]{1,0:T(8,128)(2,1)}, u32[]{:S(2)}, u32[]{:S(2)}) collective-permute-start(bf16[768,768]{1,0:T(8,128)(2,1)} %pad_maximum_fusion.3), channel_id=1, source_target_pairs={{0,1},{3,2},{4,5},{7,6},{8,9},{11,10},{12,13},{15,14},{16,17},{19,... | collective-permute-start | bytes 3538952 | tf_op jit(solution)/shard_map/ppermute | solution.py:351
  279.7 19.1 %collective-permute-done.44 = bf16[768,768]{1,0:T(8,128)(2,1)} collective-permute-done((bf16[768,768]{1,0:T(8,128)(2,1)}, bf16[768,768]{1,0:T(8,128)(2,1)}, u32[]{:S(2)}, u32[]{:S(2)}) %collective-permute-start.44) | collective-permute-done | bytes 1179680 | tf_op jit(solution)/shard_map/ppermute | solution.py:351
  304.9 5.2 %collective-permute-done.36 = bf16[128,768]{1,0:T(8,128)(2,1)S(1)} collective-permute-done((bf16[128,768]{1,0:T(8,128)(2,1)S(1)}, bf16[128,768]{1,0:T(8,128)(2,1)S(1)}, u32[]{:S(2)}, u32[]{:S(2)}) %collective-permute-start.36) | collective-permute-done | bytes 196640 | tf_op jit(solution)/shard_map/ppermute | solution.py:18
  310.1 5.8 %collective-permute-start.47 = (bf16[384,768]{1,0:T(8,128)(2,1)S(1)}, bf16[384,768]{1,0:T(8,128)(2,1)S(1)}, u32[]{:S(2)}, u32[]{:S(2)}) collective-permute-start(bf16[384,768]{1,0:T(8,128)(2,1)S(1)} %pad_maximum_fusion.17), channel_id=1, source_target_pairs={{0,1},{3,2},{4,5},{7,6},{8,9},{11,10},{12,13},{15,14},{16,17},{19,... | collective-permute-start | bytes 1769480 | tf_op jit(solution)/shard_map/ppermute | solution.py:351
  316.9 7.9 %collective-permute-done.49 = bf16[768,768]{1,0:T(8,128)(2,1)S(1)} collective-permute-done((bf16[768,768]{1,0:T(8,128)(2,1)S(1)}, bf16[768,768]{1,0:T(8,128)(2,1)S(1)}, u32[]{:S(2)}, u32[]{:S(2)}) %collective-permute-start.49) | collective-permute-done | bytes 1179680 | tf_op jit(solution)/shard_map/ppermute | solution.py:351
  333.4 10.3 %collective-permute-start.53 = (bf16[387,768]{1,0:T(8,128)(2,1)S(1)}, bf16[387,768]{1,0:T(8,128)(2,1)S(1)}, u32[]{:S(2)}, u32[]{:S(2)}) collective-permute-start(bf16[387,768]{1,0:T(8,128)(2,1)S(1)} %pad_maximum_fusion.11), channel_id=1, source_target_pairs={{0,1},{3,2},{4,5},{7,6},{8,9},{11,10},{12,13},{15,14},{16,17},{19,... | collective-permute-start | bytes 1783304 | tf_op jit(solution)/shard_map/ppermute | solution.py:351
  343.6 18.4 %collective-permute-done.55 = bf16[768,768]{1,0:T(8,128)(2,1)S(1)} collective-permute-done((bf16[768,768]{1,0:T(8,128)(2,1)S(1)}, bf16[768,768]{1,0:T(8,128)(2,1)S(1)}, u32[]{:S(2)}, u32[]{:S(2)}) %collective-permute-start.55) | collective-permute-done | bytes 1179680 | tf_op jit(solution)/shard_map/ppermute | solution.py:351
  366.6 12.9 %collective-permute-done.57 = bf16[384,768]{1,0:T(8,128)(2,1)S(1)} collective-permute-done((bf16[384,768]{1,0:T(8,128)(2,1)S(1)}, bf16[384,768]{1,0:T(8,128)(2,1)S(1)}, u32[]{:S(2)}, u32[]{:S(2)}) %collective-permute-start.57) | collective-permute-done | bytes 589856 | tf_op jit(solution)/shard_map/ppermute | solution.py:351
  381.3 14.1 %collective-permute-done.58 = bf16[387,768]{1,0:T(8,128)(2,1)S(1)} collective-permute-done((bf16[387,768]{1,0:T(8,128)(2,1)S(1)}, bf16[387,768]{1,0:T(8,128)(2,1)S(1)}, u32[]{:S(2)}, u32[]{:S(2)}) %collective-permute-start.58) | collective-permute-done | bytes 594464 | tf_op jit(solution)/shard_map/ppermute | solution.py:351
  (520 shorter events, 142.0 us)
Async XLA Ops:
  8.5 28.5 %collective-permute-start = (bf16[128,768]{1,0:T(8,128)(2,1)}, bf16[128,768]{1,0:T(8,128)(2,1)}, u32[]{:S(2)}, u32[]{:S(2)}) collective-permute-start(bf16[128,768]{1,0:T(8,128)(2,1)} %dynamic-slice_bitcast_fusion.5), channel_id=1, source_target_pairs={{0,8},{4,12},{8,0},{12,4},{1,9},{5,13},{9,1},{13,5},{2,10},{6,14},... | collective-permute-start | bytes 589832 | tf_op jit(solution)/shard_map/ppermute | solution.py:18
  11.0 37.4 %collective-permute-start.5 = (bf16[192,2304]{1,0:T(8,128)(2,1)}, bf16[192,2304]{1,0:T(8,128)(2,1)}, u32[]{:S(2)}, u32[]{:S(2)}) collective-permute-start(bf16[192,2304]{1,0:T(8,128)(2,1)} %bitcast.197), channel_id=1, source_target_pairs={{0,8},{4,12},{8,0},{12,4},{1,9},{5,13},{9,1},{13,5},{2,10},{6,14},... | collective-permute-start | bytes 2654216 | tf_op jit(solution)/shard_map/ppermute | solution.py:18
  14.0 28.1 %collective-permute-start.4 = (bf16[192,1152]{1,0:T(8,128)(2,1)}, bf16[192,1152]{1,0:T(8,128)(2,1)}, u32[]{:S(2)}, u32[]{:S(2)}) collective-permute-start(bf16[192,1152]{1,0:T(8,128)(2,1)} %pad_maximum_fusion.19), channel_id=1, source_target_pairs={{0,4},{4,0},{8,12},{12,8},{1,5},{5,1},{9,13},{13,9},{2,6},{6,2},{1... | collective-permute-start | bytes 1327112 | tf_op jit(solution)/shard_map/ppermute | solution.py:22
  15.2 23.4 %collective-permute-start.13 = (bf16[192,768]{1,0:T(8,128)(2,1)}, bf16[192,768]{1,0:T(8,128)(2,1)S(1)}, u32[]{:S(2)}, u32[]{:S(2)}) collective-permute-start(bf16[192,768]{1,0:T(8,128)(2,1)} %get-tuple-element.162), channel_id=1, source_target_pairs={{0,4},{4,0},{8,12},{12,8},{1,5},{5,1},{9,13},{13,9},{2,6},{6,2},{1... | collective-permute-start | bytes 884744 | tf_op jit(solution)/shard_map/ppermute | solution.py:22
  17.8 18.1 %collective-permute-start.3 = (bf16[2,2304]{1,0:T(2,128)(2,1)S(1)}, bf16[2,2304]{1,0:T(2,128)(2,1)S(1)}, u32[]{:S(2)}, u32[]{:S(2)}) collective-permute-start(bf16[2,2304]{1,0:T(2,128)(2,1)S(1)} %pad_maximum_fusion.25), channel_id=1, source_target_pairs={{0,8},{4,12},{8,0},{12,4},{1,9},{5,13},{9,1},{13,5},{2,10},{6,14},... | collective-permute-start | bytes 27656 | tf_op jit(solution)/shard_map/ppermute | solution.py:18
  40.3 20.8 %collective-permute-start.11 = (bf16[192,1536]{1,0:T(8,128)(2,1)}, bf16[192,1536]{1,0:T(8,128)(2,1)S(1)}, u32[]{:S(2)}, u32[]{:S(2)}) collective-permute-start(bf16[192,1536]{1,0:T(8,128)(2,1)} %get-tuple-element.64), channel_id=1, source_target_pairs={{0,8},{4,12},{8,0},{12,4},{1,9},{5,13},{9,1},{13,5},{2,10},{6,14},... | collective-permute-start | bytes 1769480 | tf_op jit(solution)/shard_map/ppermute | solution.py:18
  48.5 14.5 %collective-permute-start.8 = (bf16[192,768]{1,0:T(8,128)(2,1)S(1)}, bf16[192,768]{1,0:T(8,128)(2,1)S(1)}, u32[]{:S(2)}, u32[]{:S(2)}) collective-permute-start(bf16[192,768]{1,0:T(8,128)(2,1)S(1)} %broadcast_select_fusion.16), channel_id=1, source_target_pairs={{0,4},{4,0},{8,12},{12,8},{1,5},{5,1},{9,13},{13,9},{2,6},{6,2},{1... | collective-permute-start | bytes 884744 | tf_op jit(solution)/shard_map/ppermute | solution.py:22
  50.5 23.2 %collective-permute-start.14 = (bf16[192,1536]{1,0:T(8,128)(2,1)S(1)}, bf16[192,1536]{1,0:T(8,128)(2,1)S(1)}, u32[]{:S(2)}, u32[]{:S(2)}) collective-permute-start(bf16[192,1536]{1,0:T(8,128)(2,1)S(1)} %copy-done.82), channel_id=1, source_target_pairs={{0,8},{4,12},{8,0},{12,4},{1,9},{5,13},{9,1},{13,5},{2,10},{6,14},... | collective-permute-start | bytes 1769480 | tf_op jit(solution)/shard_map/ppermute | solution.py:18
  61.1 37.1 %collective-permute-start.12 = (bf16[192,768]{1,0:T(8,128)(2,1)S(1)}, bf16[192,768]{1,0:T(8,128)(2,1)S(1)}, u32[]{:S(2)}, u32[]{:S(2)}) collective-permute-start(bf16[192,768]{1,0:T(8,128)(2,1)S(1)} %constant_dynamic-slice_fusion.20), channel_id=1, source_target_pairs={{0,4},{4,0},{8,12},{12,8},{1,5},{5,1},{9,13},{13,9},{2,6},{6,2},{1... | collective-permute-start | bytes 884744 | tf_op jit(solution)/shard_map/ppermute | solution.py:22
  61.2 25.2 %collective-permute-start.16 = (bf16[384,768]{1,0:T(8,128)(2,1)S(1)}, bf16[384,768]{1,0:T(8,128)(2,1)S(1)}, u32[]{:S(2)}, u32[]{:S(2)}) collective-permute-start(bf16[384,768]{1,0:T(8,128)(2,1)S(1)} %copy-done.81), channel_id=1, source_target_pairs={{0,8},{4,12},{8,0},{12,4},{1,9},{5,13},{9,1},{13,5},{2,10},{6,14},... | collective-permute-start | bytes 1769480 | tf_op jit(solution)/shard_map/ppermute | solution.py:18
  63.0 35.1 %collective-permute-start.17 = (bf16[384,768]{1,0:T(8,128)(2,1)S(1)}, bf16[384,768]{1,0:T(8,128)(2,1)S(1)}, u32[]{:S(2)}, u32[]{:S(2)}) collective-permute-start(bf16[384,768]{1,0:T(8,128)(2,1)S(1)} %copy-done.80), channel_id=1, source_target_pairs={{0,8},{4,12},{8,0},{12,4},{1,9},{5,13},{9,1},{13,5},{2,10},{6,14},... | collective-permute-start | bytes 1769480 | tf_op jit(solution)/shard_map/ppermute | solution.py:18
  73.7 24.5 %collective-permute-start.15 = (bf16[192,768]{1,0:T(8,128)(2,1)S(1)}, bf16[192,768]{1,0:T(8,128)(2,1)S(1)}, u32[]{:S(2)}, u32[]{:S(2)}) collective-permute-start(bf16[192,768]{1,0:T(8,128)(2,1)S(1)} %constant_dynamic-slice_fusion.18), channel_id=1, source_target_pairs={{0,4},{4,0},{8,12},{12,8},{1,5},{5,1},{9,13},{13,9},{2,6},{6,2},{1... | collective-permute-start | bytes 884744 | tf_op jit(solution)/shard_map/ppermute | solution.py:22
  83.6 15.3 %collective-permute-start.9 = (bf16[512,768]{1,0:T(8,128)(2,1)S(1)}, bf16[512,768]{1,0:T(8,128)(2,1)S(1)}, u32[]{:S(2)}, u32[]{:S(2)}) collective-permute-start(bf16[512,768]{1,0:T(8,128)(2,1)S(1)} %get-tuple-element.63), channel_id=1, source_target_pairs={{0,4},{4,0},{8,12},{12,8},{1,5},{5,1},{9,13},{13,9},{2,6},{6,2},{1... | collective-permute-start | bytes 2359304 | tf_op jit(solution)/shard_map/ppermute | solution.py:22
  167.4 13.7 %collective-permute-start.29 = (bf16[256,768]{1,0:T(8,128)(2,1)}, bf16[256,768]{1,0:T(8,128)(2,1)}, u32[]{:S(2)}, u32[]{:S(2)}) collective-permute-start(bf16[256,768]{1,0:T(8,128)(2,1)} %fusion.37), channel_id=1, source_target_pairs={{16,0},{17,1},{18,2},{19,3},{20,4},{21,5},{22,6},{23,7},{24,8},{25... | collective-permute-start | bytes 1179656 | tf_op jit(solution)/shard_map/ppermute | solution.py:476
  194.2 29.9 %collective-permute-start.33 = (bf16[768,768]{1,0:T(8,128)(2,1)}, bf16[768,768]{1,0:T(8,128)(2,1)}, u32[]{:S(2)}, u32[]{:S(2)}) collective-permute-start(bf16[768,768]{1,0:T(8,128)(2,1)} %convolution_convert_fusion.1), channel_id=1, source_target_pairs={{0,8},{4,12},{8,0},{12,4},{1,9},{5,13},{9,1},{13,5},{2,10},{6,14},... | collective-permute-start | bytes 3538952 | tf_op jit(solution)/shard_map/ppermute | solution.py:18
  199.1 59.0 %collective-permute-start.42 = (bf16[384,768]{1,0:T(8,128)(2,1)}, bf16[384,768]{1,0:T(8,128)(2,1)}, u32[]{:S(2)}, u32[]{:S(2)}) collective-permute-start(bf16[384,768]{1,0:T(8,128)(2,1)} %convolution_convert_fusion.2), channel_id=1, source_target_pairs={{0,8},{4,12},{8,0},{12,4},{1,9},{5,13},{9,1},{13,5},{2,10},{6,14},... | collective-permute-start | bytes 1769480 | tf_op jit(solution)/shard_map/ppermute | solution.py:18
  202.2 53.9 %collective-permute-start.39 = (bf16[384,768]{1,0:T(8,128)(2,1)}, bf16[384,768]{1,0:T(8,128)(2,1)}, u32[]{:S(2)}, u32[]{:S(2)}) collective-permute-start(bf16[384,768]{1,0:T(8,128)(2,1)} %convolution_convert_fusion.3), channel_id=1, source_target_pairs={{0,8},{4,12},{8,0},{12,4},{1,9},{5,13},{9,1},{13,5},{2,10},{6,14},... | collective-permute-start | bytes 1769480 | tf_op jit(solution)/shard_map/ppermute | solution.py:18
  227.3 28.9 %collective-permute-start.40 = (bf16[768,768]{1,0:T(8,128)(2,1)}, bf16[768,768]{1,0:T(8,128)(2,1)}, u32[]{:S(2)}, u32[]{:S(2)}) collective-permute-start(bf16[768,768]{1,0:T(8,128)(2,1)} %add_convert_fusion.4), channel_id=1, source_target_pairs={{0,1},{3,2},{4,5},{7,6},{8,9},{11,10},{12,13},{15,14},{16,17},{19,... | collective-permute-start | bytes 3538952 | tf_op jit(solution)/shard_map/ppermute | solution.py:351
  233.7 65.0 %collective-permute-start.38 = (bf16[384,768]{1,0:T(8,128)(2,1)}, bf16[384,768]{1,0:T(8,128)(2,1)}, u32[]{:S(2)}, u32[]{:S(2)}) collective-permute-start(bf16[384,768]{1,0:T(8,128)(2,1)} %slice.239), channel_id=1, source_target_pairs={{0,8},{4,12},{8,0},{12,4},{1,9},{5,13},{9,1},{13,5},{2,10},{6,14},... | collective-permute-start | bytes 1769480 | tf_op jit(solution)/shard_map/ppermute | solution.py:18
  236.4 91.8 %collective-permute-start.37 = (bf16[384,768]{1,0:T(8,128)(2,1)}, bf16[384,768]{1,0:T(8,128)(2,1)}, u32[]{:S(2)}, u32[]{:S(2)}) collective-permute-start(bf16[384,768]{1,0:T(8,128)(2,1)} %maximum_maximum_fusion), channel_id=1, source_target_pairs={{0,8},{4,12},{8,0},{12,4},{1,9},{5,13},{9,1},{13,5},{2,10},{6,14},... | collective-permute-start | bytes 1769480 | tf_op jit(solution)/shard_map/ppermute | solution.py:18
  266.4 32.3 %collective-permute-start.44 = (bf16[768,768]{1,0:T(8,128)(2,1)}, bf16[768,768]{1,0:T(8,128)(2,1)}, u32[]{:S(2)}, u32[]{:S(2)}) collective-permute-start(bf16[768,768]{1,0:T(8,128)(2,1)} %pad_maximum_fusion.3), channel_id=1, source_target_pairs={{0,1},{3,2},{4,5},{7,6},{8,9},{11,10},{12,13},{15,14},{16,17},{19,... | collective-permute-start | bytes 3538952 | tf_op jit(solution)/shard_map/ppermute | solution.py:351
  276.0 26.5 %collective-permute-start.35 = (bf16[128,768]{1,0:T(8,128)(2,1)S(1)}, bf16[128,768]{1,0:T(8,128)(2,1)S(1)}, u32[]{:S(2)}, u32[]{:S(2)}) collective-permute-start(bf16[128,768]{1,0:T(8,128)(2,1)S(1)} %constant_dynamic-slice_fusion.12), channel_id=1, source_target_pairs={{0,4},{4,0},{8,12},{12,8},{1,5},{5,1},{9,13},{13,9},{2,6},{6,2},{1... | collective-permute-start | bytes 589832 | tf_op jit(solution)/shard_map/ppermute | solution.py:22
  278.2 46.5 %collective-permute-start.49 = (bf16[768,768]{1,0:T(8,128)(2,1)S(1)}, bf16[768,768]{1,0:T(8,128)(2,1)S(1)}, u32[]{:S(2)}, u32[]{:S(2)}) collective-permute-start(bf16[768,768]{1,0:T(8,128)(2,1)S(1)} %add_convert_fusion.1), channel_id=1, source_target_pairs={{1,0},{2,3},{5,4},{6,7},{9,8},{10,11},{13,12},{14,15},{17,16},{18,... | collective-permute-start | bytes 3538952 | tf_op jit(solution)/shard_map/ppermute | solution.py:351
  301.7 24.6 %collective-permute-start.48 = (bf16[768,768]{1,0:T(8,128)(2,1)S(1)}, bf16[768,768]{1,0:T(8,128)(2,1)S(1)}, u32[]{:S(2)}, u32[]{:S(2)}) collective-permute-start(bf16[768,768]{1,0:T(8,128)(2,1)S(1)} %add_convert_fusion.2), channel_id=1, source_target_pairs={{1,2},{2,1},{5,6},{6,5},{9,10},{10,9},{13,14},{14,13},{17,18},{18,... | collective-permute-start | bytes 3538952 | tf_op jit(solution)/shard_map/ppermute | solution.py:351
  303.5 28.3 %collective-permute-start.52 = (bf16[3,768]{1,0:T(4,128)(2,1)S(1)}, bf16[3,768]{1,0:T(4,128)(2,1)S(1)}, u32[]{:S(2)}, u32[]{:S(2)}) collective-permute-start(bf16[3,768]{1,0:T(4,128)(2,1)S(1)} %fusion.91), channel_id=1, source_target_pairs={{0,8},{4,12},{8,0},{12,4},{1,9},{5,13},{9,1},{13,5},{2,10},{6,14},... | collective-permute-start | bytes 13832 | tf_op jit(solution)/shard_map/ppermute | solution.py:18
  310.1 17.8 %collective-permute-start.47 = (bf16[384,768]{1,0:T(8,128)(2,1)S(1)}, bf16[384,768]{1,0:T(8,128)(2,1)S(1)}, u32[]{:S(2)}, u32[]{:S(2)}) collective-permute-start(bf16[384,768]{1,0:T(8,128)(2,1)S(1)} %pad_maximum_fusion.17), channel_id=1, source_target_pairs={{0,1},{3,2},{4,5},{7,6},{8,9},{11,10},{12,13},{15,14},{16,17},{19,... | collective-permute-start | bytes 1769480 | tf_op jit(solution)/shard_map/ppermute | solution.py:351
  328.2 33.8 %collective-permute-start.55 = (bf16[768,768]{1,0:T(8,128)(2,1)S(1)}, bf16[768,768]{1,0:T(8,128)(2,1)S(1)}, u32[]{:S(2)}, u32[]{:S(2)}) collective-permute-start(bf16[768,768]{1,0:T(8,128)(2,1)S(1)} %add_convert_fusion), channel_id=1, source_target_pairs={{1,0},{2,3},{5,4},{6,7},{9,8},{10,11},{13,12},{14,15},{17,16},{18,... | collective-permute-start | bytes 3538952 | tf_op jit(solution)/shard_map/ppermute | solution.py:351
  329.8 32.3 %collective-permute-start.54 = (bf16[384,768]{1,0:T(8,128)(2,1)S(1)}, bf16[384,768]{1,0:T(8,128)(2,1)S(1)}, u32[]{:S(2)}, u32[]{:S(2)}) collective-permute-start(bf16[384,768]{1,0:T(8,128)(2,1)S(1)} %add_convert_fusion.11), channel_id=1, source_target_pairs={{1,2},{2,1},{5,6},{6,5},{9,10},{10,9},{13,14},{14,13},{17,18},{18,... | collective-permute-start | bytes 1769480 | tf_op jit(solution)/shard_map/ppermute | solution.py:351
  333.4 29.0 %collective-permute-start.53 = (bf16[387,768]{1,0:T(8,128)(2,1)S(1)}, bf16[387,768]{1,0:T(8,128)(2,1)S(1)}, u32[]{:S(2)}, u32[]{:S(2)}) collective-permute-start(bf16[387,768]{1,0:T(8,128)(2,1)S(1)} %pad_maximum_fusion.11), channel_id=1, source_target_pairs={{0,1},{3,2},{4,5},{7,6},{8,9},{11,10},{12,13},{15,14},{16,17},{19,... | collective-permute-start | bytes 1783304 | tf_op jit(solution)/shard_map/ppermute | solution.py:351
  362.6 17.1 %collective-permute-start.56 = (bf16[387,768]{1,0:T(8,128)(2,1)S(1)}, bf16[387,768]{1,0:T(8,128)(2,1)S(1)}, u32[]{:S(2)}, u32[]{:S(2)}) collective-permute-start(bf16[387,768]{1,0:T(8,128)(2,1)S(1)} %add_convert_fusion.9), channel_id=1, source_target_pairs={{1,2},{2,1},{5,6},{6,5},{9,10},{10,9},{13,14},{14,13},{17,18},{18,... | collective-permute-start | bytes 1783304 | tf_op jit(solution)/shard_map/ppermute | solution.py:351
  363.3 16.2 %collective-permute-start.57 = (bf16[384,768]{1,0:T(8,128)(2,1)S(1)}, bf16[384,768]{1,0:T(8,128)(2,1)S(1)}, u32[]{:S(2)}, u32[]{:S(2)}) collective-permute-start(bf16[384,768]{1,0:T(8,128)(2,1)S(1)} %add_convert_fusion.10), channel_id=1, source_target_pairs={{1,0},{2,3},{5,4},{6,7},{9,8},{10,11},{13,12},{14,15},{17,16},{18,... | collective-permute-start | bytes 1769480 | tf_op jit(solution)/shard_map/ppermute | solution.py:351
  379.8 15.6 %collective-permute-start.58 = (bf16[387,768]{1,0:T(8,128)(2,1)S(1)}, bf16[387,768]{1,0:T(8,128)(2,1)S(1)}, u32[]{:S(2)}, u32[]{:S(2)}) collective-permute-start(bf16[387,768]{1,0:T(8,128)(2,1)S(1)} %add_convert_fusion.8), channel_id=1, source_target_pairs={{1,0},{2,3},{5,4},{6,7},{9,8},{10,11},{13,12},{14,15},{17,16},{18,... | collective-permute-start | bytes 1783304 | tf_op jit(solution)/shard_map/ppermute | solution.py:351
  (137 other events, 1349.2 us)
where the time goes:
time: 405 us; the launch traced here: 399 us
  waiting for transfers between devices  166 us (41%)
  starting transfers between devices  70 us (17%)
  other arithmetic  51.3 us (13%)
  Pallas kernels  44 us (11%)
  local copies, waits for them, and re-layouts  34.9 us (9%)
  matrix products  29.5 us (7%)
    ppermute x12, waiting for transfers between devices, run(): lax.ppermute(value, 'replica', self.HOPS[stage])  90.6 us
    ppermute x17, waiting for transfers between devices, across(): return lax.ppermute(value, 'fsdp', [(i, i ^ 2) for i in range(4)])  58.5 us
    pallas_call x5, Pallas kernels, call(): pl.pallas_call(kernel, out_shape=tuple(outs), in_specs=[pl.BlockSpec(memo...  44 us
    ppermute x12, starting transfers between devices, run(): lax.ppermute(value, 'replica', self.HOPS[stage])  37.3 us
    ppermute x17, starting transfers between devices, across(): return lax.ppermute(value, 'fsdp', [(i, i ^ 2) for i in range(4)])  21 us
    dot_general x9, matrix products, t_matmul(): lax.dot_general(left, right, (((0,), (0,)), ((), ())), preferred_element_...  15.7 us
    unnamed x217, local copies, waits for them, and re-layouts  14.6 us
    dot_general x12, matrix products, matmul(): return jnp.dot(left, right, preferred_element_type=F32)  10.6 us
  transfers between devices with their start and end apart: 59, of which 22 were waited for; matrix products, arithmetic and copies ran while one was open for 18% of the time, Pallas kernels for 10%

commit v1 on v0

--- a/solution.py
+++ b/solution.py
@@ -315,7 +315,7 @@
         self.results = {}
         self.last = None
         stages = 4 if self.line else 1
-        self.events = sorted((p + s, -s, p) for p in range(count) for s in range(stages))
+        self.events = sorted((p + s, -(s % 3), p, s) for p in range(count) for s in range(stages))
 
     def chained(self, value):
         if self.last is not None:
@@ -329,8 +329,7 @@
 
     def run(self, until=None):
         while self.events:
-            _, stage, piece = self.events.pop(0)
-            stage = -stage
+            _, _, piece, stage = self.events.pop(0)
             if stage == 0:
                 sides, after = self.values[piece]
                 totals = [mine.astype(F32) + self.chained(got).astype(F32) for mine, got in sides]
@@ -414,7 +413,7 @@
     got_qkv = across(qkv_weight[0])
     qkv = joined(chip, own_qkv, rows_of(got_qkv, half))
 
-    got_out = tied(across(tied(out_weight[0], first)), got_qkv)
+    got_out = tied(across(tied(out_weight[0], pair)), got_qkv)
     same = chip == core
     out = joined(
         core,
@@ -423,7 +422,7 @@
     )
 
     own, other = (part_of(up_weight[0], place, 2 * group, 1) for place in (chip, 1 - chip))
-    got_up = tied(across(tied(other, first)), got_out)
+    got_up = tied(across(tied(other, pair)), got_out)
     got_other = tied(across(tied(own, got_qkv)), got_up)
     got_down = tied(across(tied(down_weight[0][: group // 2], got_out)), got_other)
     got_last = tied(across(tied(down_weight[0][group // 2 :], got_up)), got_down)

time: 405 us -> 398 us (0.983)
  no operation moved by 1% of the time
where the time goes in v1:
time: 398 us; the launch traced here: 392 us
  waiting for transfers between devices  163 us (41%)
  starting transfers between devices  66.8 us (17%)
  other arithmetic  51.3 us (13%)
  Pallas kernels  44 us (11%)
  local copies, waits for them, and re-layouts  34.9 us (9%)
  matrix products  29.5 us (7%)
    ppermute x12, waiting for transfers between devices, run(): lax.ppermute(value, 'replica', self.HOPS[stage])  88.6 us
    ppermute x17, waiting for transfers between devices, across(): return lax.ppermute(value, 'fsdp', [(i, i ^ 2) for i in range(4)])  57.8 us
    pallas_call x5, Pallas kernels, call(): pl.pallas_call(kernel, out_shape=tuple(outs), in_specs=[pl.BlockSpec(memo...  44 us
    ppermute x12, starting transfers between devices, run(): lax.ppermute(value, 'replica', self.HOPS[stage])  35.1 us
    ppermute x17, starting transfers between devices, across(): return lax.ppermute(value, 'fsdp', [(i, i ^ 2) for i in range(4)])  20.6 us
    dot_general x9, matrix products, t_matmul(): lax.dot_general(left, right, (((0,), (0,)), ((), ())), preferred_element_...  15.7 us
    unnamed x217, local copies, waits for them, and re-layouts  14.5 us
    dot_general x12, matrix products, matmul(): return jnp.dot(left, right, preferred_element_type=F32)  10.6 us
  transfers between devices with their start and end apart: 59, of which 22 were waited for; matrix products, arithmetic and copies ran while one was open for 18% of the time, Pallas kernels for 10%

profile of v1, /device:TPU:0, one launch (start us, length us, event | category | flops | bytes accessed | tf_op | source)
XLA Modules:
  0.0 392.0 jit_solution(2126679915051744391)
XLA Ops:
  8.5 2.5 collective-permute-start
  20.1 15.9 %collective-permute-done.3 = bf16[2,2304]{1,0:T(2,128)(2,1)S(1)} collective-permute-done((bf16[2,2304]{1,0:T(2,128)(2,1)S(1)}, bf16[2,2304]{1,0:T(2,128)(2,1)S(1)}, u32[]{:S(2)}, u32[]{:S(2)}) %collective-permute-start.3) | collective-permute-done | bytes 9248 | tf_op jit(solution)/shard_map/ppermute | solution.py:18
  43.1 3.8 collective-permute-done.7
  50.7 8.8 %collective-permute-done.11 = bf16[192,1536]{1,0:T(8,128)(2,1)S(1)} collective-permute-done((bf16[192,1536]{1,0:T(8,128)(2,1)}, bf16[192,1536]{1,0:T(8,128)(2,1)S(1)}, u32[]{:S(2)}, u32[]{:S(2)}) %collective-permute-start.11) | collective-permute-done | bytes 589856 | tf_op jit(solution)/shard_map/ppermute | solution.py:18
  62.5 9.7 %collective-permute-done.14 = bf16[192,1536]{1,0:T(8,128)(2,1)S(1)} collective-permute-done((bf16[192,1536]{1,0:T(8,128)(2,1)S(1)}, bf16[192,1536]{1,0:T(8,128)(2,1)S(1)}, u32[]{:S(2)}, u32[]{:S(2)}) %collective-permute-start.14) | collective-permute-done | bytes 589856 | tf_op jit(solution)/shard_map/ppermute | solution.py:18
  72.3 9.8 %shard_map.254 = (bf16[512,768]{1,0:T(8,128)(2,1)S(1)}, bf16[512,768]{1,0:T(8,128)(2,1)}, bf16[512,1152]{1,0:T(8,128)(2,1)}, bf16[512,384]{1,0:T(8,128)(2,1)}, bf16[3,4,256,512]{3,2,1,0:T(8,128)(2,1)}) custom-call(bf16[512,768]{1,0:T(8,128)(2,1)S(1)} %bitcast.191, s32[512,1]{1,0:T(8,128)S(1)} %copy.38.seg_col, s32[1,512]{1,0:T(1,128)S(1)} %get-tuple-element.256.seg_row, ...), custom_call_target="tpu_custom_call" | custom-call | flops 2013265920 | bytes 9452032 | tf_op jit(solution)/shard_map/pallas_call | solution.py:119
  82.5 2.2 collective-permute-done.16
  84.8 12.3 %collective-permute-done.17 = bf16[384,768]{1,0:T(8,128)(2,1)S(1)} collective-permute-done((bf16[384,768]{1,0:T(8,128)(2,1)S(1)}, bf16[384,768]{1,0:T(8,128)(2,1)S(1)}, u32[]{:S(2)}, u32[]{:S(2)}) %collective-permute-start.17) | collective-permute-done | bytes 589856 | tf_op jit(solution)/shard_map/ppermute | solution.py:18
  107.0 2.4 add_convert_fusion.15
  109.4 4.4 %collective-permute-start.19 = (bf16[256,768]{1,0:T(8,128)(2,1)}, bf16[256,768]{1,0:T(8,128)(2,1)}, u32[]{:S(2)}, u32[]{:S(2)}) collective-permute-start(bf16[256,768]{1,0:T(8,128)(2,1)} %add_convert_fusion.15), channel_id=1, source_target_pairs={{0,16},{1,17},{2,18},{3,19},{4,20},{5,21},{6,22},{7,23},{8,24},{9,... | collective-permute-start | bytes 1179656 | tf_op jit(solution)/shard_map/ppermute | solution.py:459
  118.3 3.6 collective-permute-done.19
  127.3 7.3 %shard_map.255 = (bf16[512,768]{1,0:T(8,128)(2,1)S(1)}, bf16[512,768]{1,0:T(8,128)(2,1)S(1)}, bf16[512,1152]{1,0:T(8,128)(2,1)S(1)}, bf16[512,384]{1,0:T(8,128)(2,1)S(1)}, bf16[3,4,256,512]{3,2,1,0:T(8,128)(2,1)S(1)}) custom-call(bf16[512,768]{1,0:T(8,128)(2,1)S(1)} %maximum_select_fusion.hidden, s32[512,1]{1,0:T(8,128)S(1)} %copy-done.22, ...), custom_call_target="tpu_custom_call" | custom-call | flops 2013265920 | bytes 9452032 | tf_op jit(solution)/shard_map/pallas_call | solution.py:119
  144.2 3.5 shard_map.256.own
  150.1 12.0 %shard_map.257 = (f32[512,768]{1,0:T(8,128)S(1)}, bf16[512,768]{1,0:T(8,128)(2,1)}, bf16[512,1152]{1,0:T(8,128)(2,1)}, bf16[512,768]{1,0:T(8,128)(2,1)S(1)}, f32[8,768]{1,0:T(8,128)}) custom-call(bf16[512,768]{1,0:T(8,128)(2,1)S(1)} %shard_map.256.own, bf16[512,768]{1,0:T(8,128)(2,1)S(1)} %collective-permute-done.25.other, bf16[512,768]{1,0:T(8,128)(2,1)S(1)} %bitcast.193, ...), custom_call_target="tpu_custom_call" | custom-call | flops 2818572288 | bytes 14969856 | tf_op jit(solution)/shard_map/pallas_call | solution.py:119
  171.9 8.0 %collective-permute-done.29 = bf16[256,768]{1,0:T(8,128)(2,1)} collective-permute-done((bf16[256,768]{1,0:T(8,128)(2,1)}, bf16[256,768]{1,0:T(8,128)(2,1)}, u32[]{:S(2)}, u32[]{:S(2)}) %collective-permute-start.29) | collective-permute-done | bytes 393248 | tf_op jit(solution)/shard_map/ppermute | solution.py:475
  195.3 2.7 convolution_convert_fusion.3
  198.5 2.6 convolution_convert_fusion.2
  205.7 11.4 %shard_map.258 = (f32[512,768]{1,0:T(8,128)S(1)}, bf16[512,768]{1,0:T(8,128)(2,1)S(1)}, bf16[512,1152]{1,0:T(8,128)(2,1)S(1)}, bf16[512,768]{1,0:T(8,128)(2,1)S(1)}, f32[8,768]{1,0:T(8,128)S(1)}) custom-call(bf16[512,768]{1,0:T(8,128)(2,1)S(1)} %copy-done.18, bf16[512,768]{1,0:T(8,128)(2,1)} %collective-permute-done.31.other, ...), custom_call_target="tpu_custom_call" | custom-call | flops 2818572288 | bytes 14969856 | tf_op jit(solution)/shard_map/pallas_call | solution.py:119
  223.0 3.2 add_convert_fusion.4
  226.1 4.5 %collective-permute-start.38 = (bf16[768,768]{1,0:T(8,128)(2,1)}, bf16[768,768]{1,0:T(8,128)(2,1)}, u32[]{:S(2)}, u32[]{:S(2)}) collective-permute-start(bf16[768,768]{1,0:T(8,128)(2,1)} %add_convert_fusion.4), channel_id=1, source_target_pairs={{0,1},{3,2},{4,5},{7,6},{8,9},{11,10},{12,13},{15,14},{16,17},{19,... | collective-permute-start | bytes 3538952 | tf_op jit(solution)/shard_map/ppermute | solution.py:350
  238.4 16.6 %collective-permute-done.38 = bf16[768,768]{1,0:T(8,128)(2,1)} collective-permute-done((bf16[768,768]{1,0:T(8,128)(2,1)}, bf16[768,768]{1,0:T(8,128)(2,1)}, u32[]{:S(2)}, u32[]{:S(2)}) %collective-permute-start.38) | collective-permute-done | bytes 1179680 | tf_op jit(solution)/shard_map/ppermute | solution.py:350
  259.3 2.9 add_convert_fusion.3
  265.3 7.3 %collective-permute-start.46 = (bf16[768,768]{1,0:T(8,128)(2,1)}, bf16[768,768]{1,0:T(8,128)(2,1)}, u32[]{:S(2)}, u32[]{:S(2)}) collective-permute-start(bf16[768,768]{1,0:T(8,128)(2,1)} %pad_maximum_fusion.3), channel_id=1, source_target_pairs={{0,1},{3,2},{4,5},{7,6},{8,9},{11,10},{12,13},{15,14},{16,17},{19,... | collective-permute-start | bytes 3538952 | tf_op jit(solution)/shard_map/ppermute | solution.py:350
  278.5 19.1 %collective-permute-done.46 = bf16[768,768]{1,0:T(8,128)(2,1)} collective-permute-done((bf16[768,768]{1,0:T(8,128)(2,1)}, bf16[768,768]{1,0:T(8,128)(2,1)}, u32[]{:S(2)}, u32[]{:S(2)}) %collective-permute-start.46) | collective-permute-done | bytes 1179680 | tf_op jit(solution)/shard_map/ppermute | solution.py:350
  303.9 5.2 %collective-permute-done.36 = bf16[128,768]{1,0:T(8,128)(2,1)S(1)} collective-permute-done((bf16[128,768]{1,0:T(8,128)(2,1)S(1)}, bf16[128,768]{1,0:T(8,128)(2,1)S(1)}, u32[]{:S(2)}, u32[]{:S(2)}) %collective-permute-start.36) | collective-permute-done | bytes 196640 | tf_op jit(solution)/shard_map/ppermute | solution.py:18
  309.1 6.0 %collective-permute-start.48 = (bf16[384,768]{1,0:T(8,128)(2,1)S(1)}, bf16[384,768]{1,0:T(8,128)(2,1)S(1)}, u32[]{:S(2)}, u32[]{:S(2)}) collective-permute-start(bf16[384,768]{1,0:T(8,128)(2,1)S(1)} %pad_maximum_fusion.17), channel_id=1, source_target_pairs={{0,1},{3,2},{4,5},{7,6},{8,9},{11,10},{12,13},{15,14},{16,17},{19,... | collective-permute-start | bytes 1769480 | tf_op jit(solution)/shard_map/ppermute | solution.py:350
  316.5 11.0 %collective-permute-done.48 = bf16[384,768]{1,0:T(8,128)(2,1)S(1)} collective-permute-done((bf16[384,768]{1,0:T(8,128)(2,1)S(1)}, bf16[384,768]{1,0:T(8,128)(2,1)S(1)}, u32[]{:S(2)}, u32[]{:S(2)}) %collective-permute-start.48) | collective-permute-done | bytes 589856 | tf_op jit(solution)/shard_map/ppermute | solution.py:350
  331.1 7.9 %collective-permute-start.53 = (bf16[387,768]{1,0:T(8,128)(2,1)S(1)}, bf16[387,768]{1,0:T(8,128)(2,1)S(1)}, u32[]{:S(2)}, u32[]{:S(2)}) collective-permute-start(bf16[387,768]{1,0:T(8,128)(2,1)S(1)} %pad_maximum_fusion.11), channel_id=1, source_target_pairs={{0,1},{3,2},{4,5},{7,6},{8,9},{11,10},{12,13},{15,14},{16,17},{19,... | collective-permute-start | bytes 1783304 | tf_op jit(solution)/shard_map/ppermute | solution.py:350
  342.1 10.1 %collective-permute-done.53 = bf16[387,768]{1,0:T(8,128)(2,1)S(1)} collective-permute-done((bf16[387,768]{1,0:T(8,128)(2,1)S(1)}, bf16[387,768]{1,0:T(8,128)(2,1)S(1)}, u32[]{:S(2)}, u32[]{:S(2)}) %collective-permute-start.53) | collective-permute-done | bytes 594464 | tf_op jit(solution)/shard_map/ppermute | solution.py:350
  353.1 10.6 %collective-permute-done.56 = bf16[768,768]{1,0:T(8,128)(2,1)S(1)} collective-permute-done((bf16[768,768]{1,0:T(8,128)(2,1)S(1)}, bf16[768,768]{1,0:T(8,128)(2,1)S(1)}, u32[]{:S(2)}, u32[]{:S(2)}) %collective-permute-start.56) | collective-permute-done | bytes 1179680 | tf_op jit(solution)/shard_map/ppermute | solution.py:350
  367.4 8.9 %collective-permute-done.58 = bf16[384,768]{1,0:T(8,128)(2,1)S(1)} collective-permute-done((bf16[384,768]{1,0:T(8,128)(2,1)S(1)}, bf16[384,768]{1,0:T(8,128)(2,1)S(1)}, u32[]{:S(2)}, u32[]{:S(2)}) %collective-permute-start.58) | collective-permute-done | bytes 589856 | tf_op jit(solution)/shard_map/ppermute | solution.py:350
  376.6 12.2 %collective-permute-done.57 = bf16[387,768]{1,0:T(8,128)(2,1)S(1)} collective-permute-done((bf16[387,768]{1,0:T(8,128)(2,1)S(1)}, bf16[387,768]{1,0:T(8,128)(2,1)S(1)}, u32[]{:S(2)}, u32[]{:S(2)}) %collective-permute-start.57) | collective-permute-done | bytes 594464 | tf_op jit(solution)/shard_map/ppermute | solution.py:350
  (520 shorter events, 140.7 us)
Async XLA Ops:
  8.5 28.5 %collective-permute-start = (bf16[128,768]{1,0:T(8,128)(2,1)}, bf16[128,768]{1,0:T(8,128)(2,1)}, u32[]{:S(2)}, u32[]{:S(2)}) collective-permute-start(bf16[128,768]{1,0:T(8,128)(2,1)} %dynamic-slice_bitcast_fusion.5), channel_id=1, source_target_pairs={{0,8},{4,12},{8,0},{12,4},{1,9},{5,13},{9,1},{13,5},{2,10},{6,14},... | collective-permute-start | bytes 589832 | tf_op jit(solution)/shard_map/ppermute | solution.py:18
  11.0 35.8 %collective-permute-start.5 = (bf16[192,2304]{1,0:T(8,128)(2,1)}, bf16[192,2304]{1,0:T(8,128)(2,1)}, u32[]{:S(2)}, u32[]{:S(2)}) collective-permute-start(bf16[192,2304]{1,0:T(8,128)(2,1)} %bitcast.197), channel_id=1, source_target_pairs={{0,8},{4,12},{8,0},{12,4},{1,9},{5,13},{9,1},{13,5},{2,10},{6,14},... | collective-permute-start | bytes 2654216 | tf_op jit(solution)/shard_map/ppermute | solution.py:18
  14.0 27.7 %collective-permute-start.4 = (bf16[192,1152]{1,0:T(8,128)(2,1)}, bf16[192,1152]{1,0:T(8,128)(2,1)}, u32[]{:S(2)}, u32[]{:S(2)}) collective-permute-start(bf16[192,1152]{1,0:T(8,128)(2,1)} %pad_maximum_fusion.19), channel_id=1, source_target_pairs={{0,4},{4,0},{8,12},{12,8},{1,5},{5,1},{9,13},{13,9},{2,6},{6,2},{1... | collective-permute-start | bytes 1327112 | tf_op jit(solution)/shard_map/ppermute | solution.py:22
  15.2 24.6 %collective-permute-start.13 = (bf16[192,768]{1,0:T(8,128)(2,1)}, bf16[192,768]{1,0:T(8,128)(2,1)S(1)}, u32[]{:S(2)}, u32[]{:S(2)}) collective-permute-start(bf16[192,768]{1,0:T(8,128)(2,1)} %get-tuple-element.162), channel_id=1, source_target_pairs={{0,4},{4,0},{8,12},{12,8},{1,5},{5,1},{9,13},{13,9},{2,6},{6,2},{1... | collective-permute-start | bytes 884744 | tf_op jit(solution)/shard_map/ppermute | solution.py:22
  17.8 18.1 %collective-permute-start.3 = (bf16[2,2304]{1,0:T(2,128)(2,1)S(1)}, bf16[2,2304]{1,0:T(2,128)(2,1)S(1)}, u32[]{:S(2)}, u32[]{:S(2)}) collective-permute-start(bf16[2,2304]{1,0:T(2,128)(2,1)S(1)} %pad_maximum_fusion.25), channel_id=1, source_target_pairs={{0,8},{4,12},{8,0},{12,4},{1,9},{5,13},{9,1},{13,5},{2,10},{6,14},... | collective-permute-start | bytes 27656 | tf_op jit(solution)/shard_map/ppermute | solution.py:18
  39.8 19.7 %collective-permute-start.11 = (bf16[192,1536]{1,0:T(8,128)(2,1)}, bf16[192,1536]{1,0:T(8,128)(2,1)S(1)}, u32[]{:S(2)}, u32[]{:S(2)}) collective-permute-start(bf16[192,1536]{1,0:T(8,128)(2,1)} %get-tuple-element.64), channel_id=1, source_target_pairs={{0,8},{4,12},{8,0},{12,4},{1,9},{5,13},{9,1},{13,5},{2,10},{6,14},... | collective-permute-start | bytes 1769480 | tf_op jit(solution)/shard_map/ppermute | solution.py:18
  46.9 14.5 %collective-permute-start.8 = (bf16[192,768]{1,0:T(8,128)(2,1)S(1)}, bf16[192,768]{1,0:T(8,128)(2,1)S(1)}, u32[]{:S(2)}, u32[]{:S(2)}) collective-permute-start(bf16[192,768]{1,0:T(8,128)(2,1)S(1)} %broadcast_select_fusion.16), channel_id=1, source_target_pairs={{0,4},{4,0},{8,12},{12,8},{1,5},{5,1},{9,13},{13,9},{2,6},{6,2},{1... | collective-permute-start | bytes 884744 | tf_op jit(solution)/shard_map/ppermute | solution.py:22
  48.5 13.3 %collective-permute-start.6 = (bf16[192,1152]{1,0:T(8,128)(2,1)S(1)}, bf16[192,1152]{1,0:T(8,128)(2,1)S(1)}, u32[]{:S(2)}, u32[]{:S(2)}) collective-permute-start(bf16[192,1152]{1,0:T(8,128)(2,1)S(1)} %pad_maximum_fusion.21), channel_id=1, source_target_pairs={{0,4},{4,0},{8,12},{12,8},{1,5},{5,1},{9,13},{13,9},{2,6},{6,2},{1... | collective-permute-start | bytes 1327112 | tf_op jit(solution)/shard_map/ppermute | solution.py:22
  48.9 23.2 %collective-permute-start.14 = (bf16[192,1536]{1,0:T(8,128)(2,1)S(1)}, bf16[192,1536]{1,0:T(8,128)(2,1)S(1)}, u32[]{:S(2)}, u32[]{:S(2)}) collective-permute-start(bf16[192,1536]{1,0:T(8,128)(2,1)S(1)} %copy-done.82), channel_id=1, source_target_pairs={{0,8},{4,12},{8,0},{12,4},{1,9},{5,13},{9,1},{13,5},{2,10},{6,14},... | collective-permute-start | bytes 1769480 | tf_op jit(solution)/shard_map/ppermute | solution.py:18
  59.5 37.6 %collective-permute-start.12 = (bf16[192,768]{1,0:T(8,128)(2,1)S(1)}, bf16[192,768]{1,0:T(8,128)(2,1)S(1)}, u32[]{:S(2)}, u32[]{:S(2)}) collective-permute-start(bf16[192,768]{1,0:T(8,128)(2,1)S(1)} %constant_dynamic-slice_fusion.20), channel_id=1, source_target_pairs={{0,4},{4,0},{8,12},{12,8},{1,5},{5,1},{9,13},{13,9},{2,6},{6,2},{1... | collective-permute-start | bytes 884744 | tf_op jit(solution)/shard_map/ppermute | solution.py:22
  59.6 25.2 %collective-permute-start.16 = (bf16[384,768]{1,0:T(8,128)(2,1)S(1)}, bf16[384,768]{1,0:T(8,128)(2,1)S(1)}, u32[]{:S(2)}, u32[]{:S(2)}) collective-permute-start(bf16[384,768]{1,0:T(8,128)(2,1)S(1)} %copy-done.81), channel_id=1, source_target_pairs={{0,8},{4,12},{8,0},{12,4},{1,9},{5,13},{9,1},{13,5},{2,10},{6,14},... | collective-permute-start | bytes 1769480 | tf_op jit(solution)/shard_map/ppermute | solution.py:18
  61.4 35.6 %collective-permute-start.17 = (bf16[384,768]{1,0:T(8,128)(2,1)S(1)}, bf16[384,768]{1,0:T(8,128)(2,1)S(1)}, u32[]{:S(2)}, u32[]{:S(2)}) collective-permute-start(bf16[384,768]{1,0:T(8,128)(2,1)S(1)} %copy-done.80), channel_id=1, source_target_pairs={{0,8},{4,12},{8,0},{12,4},{1,9},{5,13},{9,1},{13,5},{2,10},{6,14},... | collective-permute-start | bytes 1769480 | tf_op jit(solution)/shard_map/ppermute | solution.py:18
  72.1 25.0 %collective-permute-start.15 = (bf16[192,768]{1,0:T(8,128)(2,1)S(1)}, bf16[192,768]{1,0:T(8,128)(2,1)S(1)}, u32[]{:S(2)}, u32[]{:S(2)}) collective-permute-start(bf16[192,768]{1,0:T(8,128)(2,1)S(1)} %constant_dynamic-slice_fusion.18), channel_id=1, source_target_pairs={{0,4},{4,0},{8,12},{12,8},{1,5},{5,1},{9,13},{13,9},{2,6},{6,2},{1... | collective-permute-start | bytes 884744 | tf_op jit(solution)/shard_map/ppermute | solution.py:22
  82.0 15.8 %collective-permute-start.9 = (bf16[512,768]{1,0:T(8,128)(2,1)S(1)}, bf16[512,768]{1,0:T(8,128)(2,1)S(1)}, u32[]{:S(2)}, u32[]{:S(2)}) collective-permute-start(bf16[512,768]{1,0:T(8,128)(2,1)S(1)} %get-tuple-element.63), channel_id=1, source_target_pairs={{0,4},{4,0},{8,12},{12,8},{1,5},{5,1},{9,13},{13,9},{2,6},{6,2},{1... | collective-permute-start | bytes 2359304 | tf_op jit(solution)/shard_map/ppermute | solution.py:22
  166.3 13.7 %collective-permute-start.29 = (bf16[256,768]{1,0:T(8,128)(2,1)}, bf16[256,768]{1,0:T(8,128)(2,1)}, u32[]{:S(2)}, u32[]{:S(2)}) collective-permute-start(bf16[256,768]{1,0:T(8,128)(2,1)} %fusion.37), channel_id=1, source_target_pairs={{16,0},{17,1},{18,2},{19,3},{20,4},{21,5},{22,6},{23,7},{24,8},{25... | collective-permute-start | bytes 1179656 | tf_op jit(solution)/shard_map/ppermute | solution.py:475
  193.1 29.9 %collective-permute-start.33 = (bf16[768,768]{1,0:T(8,128)(2,1)}, bf16[768,768]{1,0:T(8,128)(2,1)}, u32[]{:S(2)}, u32[]{:S(2)}) collective-permute-start(bf16[768,768]{1,0:T(8,128)(2,1)} %convolution_convert_fusion.1), channel_id=1, source_target_pairs={{0,8},{4,12},{8,0},{12,4},{1,9},{5,13},{9,1},{13,5},{2,10},{6,14},... | collective-permute-start | bytes 3538952 | tf_op jit(solution)/shard_map/ppermute | solution.py:18
  197.9 59.0 %collective-permute-start.40 = (bf16[384,768]{1,0:T(8,128)(2,1)}, bf16[384,768]{1,0:T(8,128)(2,1)}, u32[]{:S(2)}, u32[]{:S(2)}) collective-permute-start(bf16[384,768]{1,0:T(8,128)(2,1)} %convolution_convert_fusion.3), channel_id=1, source_target_pairs={{0,8},{4,12},{8,0},{12,4},{1,9},{5,13},{9,1},{13,5},{2,10},{6,14},... | collective-permute-start | bytes 1769480 | tf_op jit(solution)/shard_map/ppermute | solution.py:18
  201.1 53.9 %collective-permute-start.41 = (bf16[384,768]{1,0:T(8,128)(2,1)}, bf16[384,768]{1,0:T(8,128)(2,1)}, u32[]{:S(2)}, u32[]{:S(2)}) collective-permute-start(bf16[384,768]{1,0:T(8,128)(2,1)} %convolution_convert_fusion.2), channel_id=1, source_target_pairs={{0,8},{4,12},{8,0},{12,4},{1,9},{5,13},{9,1},{13,5},{2,10},{6,14},... | collective-permute-start | bytes 1769480 | tf_op jit(solution)/shard_map/ppermute | solution.py:18
  226.1 28.9 %collective-permute-start.38 = (bf16[768,768]{1,0:T(8,128)(2,1)}, bf16[768,768]{1,0:T(8,128)(2,1)}, u32[]{:S(2)}, u32[]{:S(2)}) collective-permute-start(bf16[768,768]{1,0:T(8,128)(2,1)} %add_convert_fusion.4), channel_id=1, source_target_pairs={{0,1},{3,2},{4,5},{7,6},{8,9},{11,10},{12,13},{15,14},{16,17},{19,... | collective-permute-start | bytes 3538952 | tf_op jit(solution)/shard_map/ppermute | solution.py:350
  232.6 65.0 %collective-permute-start.43 = (bf16[384,768]{1,0:T(8,128)(2,1)}, bf16[384,768]{1,0:T(8,128)(2,1)}, u32[]{:S(2)}, u32[]{:S(2)}) collective-permute-start(bf16[384,768]{1,0:T(8,128)(2,1)} %slice.239), channel_id=1, source_target_pairs={{0,8},{4,12},{8,0},{12,4},{1,9},{5,13},{9,1},{13,5},{2,10},{6,14},... | collective-permute-start | bytes 1769480 | tf_op jit(solution)/shard_map/ppermute | solution.py:18
  235.3 92.2 %collective-permute-start.37 = (bf16[384,768]{1,0:T(8,128)(2,1)}, bf16[384,768]{1,0:T(8,128)(2,1)}, u32[]{:S(2)}, u32[]{:S(2)}) collective-permute-start(bf16[384,768]{1,0:T(8,128)(2,1)} %maximum_maximum_fusion), channel_id=1, source_target_pairs={{0,8},{4,12},{8,0},{12,4},{1,9},{5,13},{9,1},{13,5},{2,10},{6,14},... | collective-permute-start | bytes 1769480 | tf_op jit(solution)/shard_map/ppermute | solution.py:18
  265.3 32.3 %collective-permute-start.46 = (bf16[768,768]{1,0:T(8,128)(2,1)}, bf16[768,768]{1,0:T(8,128)(2,1)}, u32[]{:S(2)}, u32[]{:S(2)}) collective-permute-start(bf16[768,768]{1,0:T(8,128)(2,1)} %pad_maximum_fusion.3), channel_id=1, source_target_pairs={{0,1},{3,2},{4,5},{7,6},{8,9},{11,10},{12,13},{15,14},{16,17},{19,... | collective-permute-start | bytes 3538952 | tf_op jit(solution)/shard_map/ppermute | solution.py:350
  274.8 26.7 %collective-permute-start.35 = (bf16[128,768]{1,0:T(8,128)(2,1)S(1)}, bf16[128,768]{1,0:T(8,128)(2,1)S(1)}, u32[]{:S(2)}, u32[]{:S(2)}) collective-permute-start(bf16[128,768]{1,0:T(8,128)(2,1)S(1)} %constant_dynamic-slice_fusion.12), channel_id=1, source_target_pairs={{0,4},{4,0},{8,12},{12,8},{1,5},{5,1},{9,13},{13,9},{2,6},{6,2},{1... | collective-permute-start | bytes 589832 | tf_op jit(solution)/shard_map/ppermute | solution.py:22
  277.2 50.3 %collective-permute-start.42 = (bf16[768,768]{1,0:T(8,128)(2,1)S(1)}, bf16[768,768]{1,0:T(8,128)(2,1)S(1)}, u32[]{:S(2)}, u32[]{:S(2)}) collective-permute-start(bf16[768,768]{1,0:T(8,128)(2,1)S(1)} %add_convert_fusion.2), channel_id=1, source_target_pairs={{1,0},{2,3},{5,4},{6,7},{9,8},{10,11},{13,12},{14,15},{17,16},{18,... | collective-permute-start | bytes 3538952 | tf_op jit(solution)/shard_map/ppermute | solution.py:350
  299.3 16.9 %collective-permute-start.49 = (bf16[768,768]{1,0:T(8,128)(2,1)S(1)}, bf16[768,768]{1,0:T(8,128)(2,1)S(1)}, u32[]{:S(2)}, u32[]{:S(2)}) collective-permute-start(bf16[768,768]{1,0:T(8,128)(2,1)S(1)} %add_convert_fusion.1), channel_id=1, source_target_pairs={{1,2},{2,1},{5,6},{6,5},{9,10},{10,9},{13,14},{14,13},{17,18},{18,... | collective-permute-start | bytes 3538952 | tf_op jit(solution)/shard_map/ppermute | solution.py:350
  303.0 24.4 %collective-permute-start.52 = (bf16[3,768]{1,0:T(4,128)(2,1)S(1)}, bf16[3,768]{1,0:T(4,128)(2,1)S(1)}, u32[]{:S(2)}, u32[]{:S(2)}) collective-permute-start(bf16[3,768]{1,0:T(4,128)(2,1)S(1)} %fusion.91), channel_id=1, source_target_pairs={{0,8},{4,12},{8,0},{12,4},{1,9},{5,13},{9,1},{13,5},{2,10},{6,14},... | collective-permute-start | bytes 13832 | tf_op jit(solution)/shard_map/ppermute | solution.py:18
  309.1 18.4 %collective-permute-start.48 = (bf16[384,768]{1,0:T(8,128)(2,1)S(1)}, bf16[384,768]{1,0:T(8,128)(2,1)S(1)}, u32[]{:S(2)}, u32[]{:S(2)}) collective-permute-start(bf16[384,768]{1,0:T(8,128)(2,1)S(1)} %pad_maximum_fusion.17), channel_id=1, source_target_pairs={{0,1},{3,2},{4,5},{7,6},{8,9},{11,10},{12,13},{15,14},{16,17},{19,... | collective-permute-start | bytes 1769480 | tf_op jit(solution)/shard_map/ppermute | solution.py:350
  329.7 33.9 %collective-permute-start.56 = (bf16[768,768]{1,0:T(8,128)(2,1)S(1)}, bf16[768,768]{1,0:T(8,128)(2,1)S(1)}, u32[]{:S(2)}, u32[]{:S(2)}) collective-permute-start(bf16[768,768]{1,0:T(8,128)(2,1)S(1)} %add_convert_fusion), channel_id=1, source_target_pairs={{1,0},{2,3},{5,4},{6,7},{9,8},{10,11},{13,12},{14,15},{17,16},{18,... | collective-permute-start | bytes 3538952 | tf_op jit(solution)/shard_map/ppermute | solution.py:350
  331.1 21.1 %collective-permute-start.53 = (bf16[387,768]{1,0:T(8,128)(2,1)S(1)}, bf16[387,768]{1,0:T(8,128)(2,1)S(1)}, u32[]{:S(2)}, u32[]{:S(2)}) collective-permute-start(bf16[387,768]{1,0:T(8,128)(2,1)S(1)} %pad_maximum_fusion.11), channel_id=1, source_target_pairs={{0,1},{3,2},{4,5},{7,6},{8,9},{11,10},{12,13},{15,14},{16,17},{19,... | collective-permute-start | bytes 1783304 | tf_op jit(solution)/shard_map/ppermute | solution.py:350
  340.8 35.5 %collective-permute-start.58 = (bf16[384,768]{1,0:T(8,128)(2,1)S(1)}, bf16[384,768]{1,0:T(8,128)(2,1)S(1)}, u32[]{:S(2)}, u32[]{:S(2)}) collective-permute-start(bf16[384,768]{1,0:T(8,128)(2,1)S(1)} %add_convert_fusion.10), channel_id=1, source_target_pairs={{1,0},{2,3},{5,4},{6,7},{9,8},{10,11},{13,12},{14,15},{17,16},{18,... | collective-permute-start | bytes 1769480 | tf_op jit(solution)/shard_map/ppermute | solution.py:350
  352.4 13.5 %collective-permute-start.55 = (bf16[387,768]{1,0:T(8,128)(2,1)S(1)}, bf16[387,768]{1,0:T(8,128)(2,1)S(1)}, u32[]{:S(2)}, u32[]{:S(2)}) collective-permute-start(bf16[387,768]{1,0:T(8,128)(2,1)S(1)} %add_convert_fusion.9), channel_id=1, source_target_pairs={{1,2},{2,1},{5,6},{6,5},{9,10},{10,9},{13,14},{14,13},{17,18},{18,... | collective-permute-start | bytes 1783304 | tf_op jit(solution)/shard_map/ppermute | solution.py:350
  366.1 22.7 %collective-permute-start.57 = (bf16[387,768]{1,0:T(8,128)(2,1)S(1)}, bf16[387,768]{1,0:T(8,128)(2,1)S(1)}, u32[]{:S(2)}, u32[]{:S(2)}) collective-permute-start(bf16[387,768]{1,0:T(8,128)(2,1)S(1)} %add_convert_fusion.8), channel_id=1, source_target_pairs={{1,0},{2,3},{5,4},{6,7},{9,8},{10,11},{13,12},{14,15},{17,16},{18,... | collective-permute-start | bytes 1783304 | tf_op jit(solution)/shard_map/ppermute | solution.py:350
  (137 other events, 1353.7 us)

commit v2 on v1

--- a/solution.py
+++ b/solution.py
@@ -487,7 +487,7 @@
 
     other = t_matmul(activated[1], grad).astype(BF16)
     sums.put(0, [(t_matmul(activated[0], grad), other)], lambda v: v)
-    g_pre, part = feed_back(grad, slopes, w)
+    g_pre, part = feed_back(tied(grad, other), slopes, w)
     stay, leave = sides(normed2)
     up_sides = [(t_matmul(stay, g_pre[i]), t_matmul(leave, g_pre[1 - i])) for i in range(2)]
     sums.put(1, up_sides, lambda a, b: jnp.concatenate([swapped(a), swapped(b)]))

time: 398 us -> 396 us (level)
    unnamed x217 -> x209, local copies, waits for them, and re-layouts: 14.5 us -> 12.8 us
  transfers between devices with their start and end apart: 59 -> 59, of which waited for: 22 -> 22; matrix products, arithmetic and copies ran while one was open for 18% -> 19% of each run, Pallas kernels for 10% -> 10%
where the time goes in v2:
time: 396 us; the launch traced here: 390 us
  waiting for transfers between devices  162 us (41%)
  starting transfers between devices  66.8 us (17%)
  other arithmetic  51.2 us (13%)
  Pallas kernels  44 us (11%)
  local copies, waits for them, and re-layouts  33.3 us (8%)
  matrix products  29.6 us (7%)
    ppermute x12, waiting for transfers between devices, run(): lax.ppermute(value, 'replica', self.HOPS[stage])  88.7 us
    ppermute x17, waiting for transfers between devices, across(): return lax.ppermute(value, 'fsdp', [(i, i ^ 2) for i in range(4)])  57.7 us
    pallas_call x5, Pallas kernels, call(): pl.pallas_call(kernel, out_shape=tuple(outs), in_specs=[pl.BlockSpec(memo...  44 us
    ppermute x12, starting transfers between devices, run(): lax.ppermute(value, 'replica', self.HOPS[stage])  35.1 us
    ppermute x17, starting transfers between devices, across(): return lax.ppermute(value, 'fsdp', [(i, i ^ 2) for i in range(4)])  20.9 us
    dot_general x9, matrix products, t_matmul(): lax.dot_general(left, right, (((0,), (0,)), ((), ())), preferred_element_...  15.7 us
    unnamed x209, local copies, waits for them, and re-layouts  12.8 us
    dot_general x12, matrix products, matmul(): return jnp.dot(left, right, preferred_element_type=F32)  10.6 us
  transfers between devices with their start and end apart: 59, of which 22 were waited for; matrix products, arithmetic and copies ran while one was open for 19% of the time, Pallas kernels for 10%

profile of v2, /device:TPU:0, one launch (start us, length us, event | category | flops | bytes accessed | tf_op | source)
XLA Modules:
  0.0 389.9 jit_solution(9829039114485175679)
XLA Ops:
  8.5 2.5 collective-permute-start
  20.1 15.8 %collective-permute-done.3 = bf16[2,2304]{1,0:T(2,128)(2,1)S(1)} collective-permute-done((bf16[2,2304]{1,0:T(2,128)(2,1)S(1)}, bf16[2,2304]{1,0:T(2,128)(2,1)S(1)}, u32[]{:S(2)}, u32[]{:S(2)}) %collective-permute-start.3) | collective-permute-done | bytes 9248 | tf_op jit(solution)/shard_map/ppermute | solution.py:18
  43.0 3.8 collective-permute-done.7
  50.7 8.8 %collective-permute-done.11 = bf16[192,1536]{1,0:T(8,128)(2,1)S(1)} collective-permute-done((bf16[192,1536]{1,0:T(8,128)(2,1)}, bf16[192,1536]{1,0:T(8,128)(2,1)S(1)}, u32[]{:S(2)}, u32[]{:S(2)}) %collective-permute-start.11) | collective-permute-done | bytes 589856 | tf_op jit(solution)/shard_map/ppermute | solution.py:18
  62.4 9.7 %collective-permute-done.14 = bf16[192,1536]{1,0:T(8,128)(2,1)S(1)} collective-permute-done((bf16[192,1536]{1,0:T(8,128)(2,1)S(1)}, bf16[192,1536]{1,0:T(8,128)(2,1)S(1)}, u32[]{:S(2)}, u32[]{:S(2)}) %collective-permute-start.14) | collective-permute-done | bytes 589856 | tf_op jit(solution)/shard_map/ppermute | solution.py:18
  72.2 9.8 %shard_map.254 = (bf16[512,768]{1,0:T(8,128)(2,1)S(1)}, bf16[512,768]{1,0:T(8,128)(2,1)}, bf16[512,1152]{1,0:T(8,128)(2,1)}, bf16[512,384]{1,0:T(8,128)(2,1)}, bf16[3,4,256,512]{3,2,1,0:T(8,128)(2,1)}) custom-call(bf16[512,768]{1,0:T(8,128)(2,1)S(1)} %bitcast.187, s32[512,1]{1,0:T(8,128)S(1)} %copy.37.seg_col, s32[1,512]{1,0:T(1,128)S(1)} %get-tuple-element.242.seg_row, ...), custom_call_target="tpu_custom_call" | custom-call | flops 2013265920 | bytes 9452032 | tf_op jit(solution)/shard_map/pallas_call | solution.py:119
  82.5 2.2 collective-permute-done.16
  84.7 12.3 %collective-permute-done.17 = bf16[384,768]{1,0:T(8,128)(2,1)S(1)} collective-permute-done((bf16[384,768]{1,0:T(8,128)(2,1)S(1)}, bf16[384,768]{1,0:T(8,128)(2,1)S(1)}, u32[]{:S(2)}, u32[]{:S(2)}) %collective-permute-start.17) | collective-permute-done | bytes 589856 | tf_op jit(solution)/shard_map/ppermute | solution.py:18
  107.0 2.4 add_convert_fusion.15
  109.3 4.4 %collective-permute-start.19 = (bf16[256,768]{1,0:T(8,128)(2,1)}, bf16[256,768]{1,0:T(8,128)(2,1)}, u32[]{:S(2)}, u32[]{:S(2)}) collective-permute-start(bf16[256,768]{1,0:T(8,128)(2,1)} %add_convert_fusion.15), channel_id=1, source_target_pairs={{0,16},{1,17},{2,18},{3,19},{4,20},{5,21},{6,22},{7,23},{8,24},{9,... | collective-permute-start | bytes 1179656 | tf_op jit(solution)/shard_map/ppermute | solution.py:459
  118.3 3.6 collective-permute-done.19
  127.3 7.3 %shard_map.255 = (bf16[512,768]{1,0:T(8,128)(2,1)S(1)}, bf16[512,768]{1,0:T(8,128)(2,1)S(1)}, bf16[512,1152]{1,0:T(8,128)(2,1)S(1)}, bf16[512,384]{1,0:T(8,128)(2,1)S(1)}, bf16[3,4,256,512]{3,2,1,0:T(8,128)(2,1)S(1)}) custom-call(bf16[512,768]{1,0:T(8,128)(2,1)S(1)} %maximum_select_fusion.hidden, s32[512,1]{1,0:T(8,128)S(1)} %copy-done.22, ...), custom_call_target="tpu_custom_call" | custom-call | flops 2013265920 | bytes 9452032 | tf_op jit(solution)/shard_map/pallas_call | solution.py:119
  144.2 3.5 shard_map.256.own
  150.1 12.0 %shard_map.257 = (f32[512,768]{1,0:T(8,128)S(1)}, bf16[512,768]{1,0:T(8,128)(2,1)}, bf16[512,1152]{1,0:T(8,128)(2,1)}, bf16[512,768]{1,0:T(8,128)(2,1)S(1)}, f32[8,768]{1,0:T(8,128)}) custom-call(bf16[512,768]{1,0:T(8,128)(2,1)S(1)} %shard_map.256.own, bf16[512,768]{1,0:T(8,128)(2,1)S(1)} %collective-permute-done.25.other, bf16[512,768]{1,0:T(8,128)(2,1)S(1)} %bitcast.186, ...), custom_call_target="tpu_custom_call" | custom-call | flops 2818572288 | bytes 14969856 | tf_op jit(solution)/shard_map/pallas_call | solution.py:119
  171.9 8.0 %collective-permute-done.29 = bf16[256,768]{1,0:T(8,128)(2,1)} collective-permute-done((bf16[256,768]{1,0:T(8,128)(2,1)}, bf16[256,768]{1,0:T(8,128)(2,1)}, u32[]{:S(2)}, u32[]{:S(2)}) %collective-permute-start.29) | collective-permute-done | bytes 393248 | tf_op jit(solution)/shard_map/ppermute | solution.py:475
  193.2 2.7 convolution_convert_fusion.3
  196.5 2.6 convolution_convert_fusion.2
  203.6 11.4 %shard_map.258 = (f32[512,768]{1,0:T(8,128)S(1)}, bf16[512,768]{1,0:T(8,128)(2,1)S(1)}, bf16[512,1152]{1,0:T(8,128)(2,1)S(1)}, bf16[512,768]{1,0:T(8,128)(2,1)S(1)}, f32[8,768]{1,0:T(8,128)S(1)}) custom-call(bf16[512,768]{1,0:T(8,128)(2,1)S(1)} %copy-done.18, bf16[512,768]{1,0:T(8,128)(2,1)} %collective-permute-done.31.other, ...), custom_call_target="tpu_custom_call" | custom-call | flops 2818572288 | bytes 14969856 | tf_op jit(solution)/shard_map/pallas_call | solution.py:119
  220.9 3.2 add_convert_fusion.4
  224.0 4.5 %collective-permute-start.38 = (bf16[768,768]{1,0:T(8,128)(2,1)}, bf16[768,768]{1,0:T(8,128)(2,1)}, u32[]{:S(2)}, u32[]{:S(2)}) collective-permute-start(bf16[768,768]{1,0:T(8,128)(2,1)} %add_convert_fusion.4), channel_id=1, source_target_pairs={{0,1},{3,2},{4,5},{7,6},{8,9},{11,10},{12,13},{15,14},{16,17},{19,... | collective-permute-start | bytes 3538952 | tf_op jit(solution)/shard_map/ppermute | solution.py:350
  236.2 16.7 %collective-permute-done.38 = bf16[768,768]{1,0:T(8,128)(2,1)} collective-permute-done((bf16[768,768]{1,0:T(8,128)(2,1)}, bf16[768,768]{1,0:T(8,128)(2,1)}, u32[]{:S(2)}, u32[]{:S(2)}) %collective-permute-start.38) | collective-permute-done | bytes 1179680 | tf_op jit(solution)/shard_map/ppermute | solution.py:350
  257.2 2.9 add_convert_fusion.3
  263.2 7.3 %collective-permute-start.46 = (bf16[768,768]{1,0:T(8,128)(2,1)}, bf16[768,768]{1,0:T(8,128)(2,1)}, u32[]{:S(2)}, u32[]{:S(2)}) collective-permute-start(bf16[768,768]{1,0:T(8,128)(2,1)} %pad_maximum_fusion.3), channel_id=1, source_target_pairs={{0,1},{3,2},{4,5},{7,6},{8,9},{11,10},{12,13},{15,14},{16,17},{19,... | collective-permute-start | bytes 3538952 | tf_op jit(solution)/shard_map/ppermute | solution.py:350
  276.4 19.2 %collective-permute-done.46 = bf16[768,768]{1,0:T(8,128)(2,1)} collective-permute-done((bf16[768,768]{1,0:T(8,128)(2,1)}, bf16[768,768]{1,0:T(8,128)(2,1)}, u32[]{:S(2)}, u32[]{:S(2)}) %collective-permute-start.46) | collective-permute-done | bytes 1179680 | tf_op jit(solution)/shard_map/ppermute | solution.py:350
  301.9 5.1 %collective-permute-done.36 = bf16[128,768]{1,0:T(8,128)(2,1)S(1)} collective-permute-done((bf16[128,768]{1,0:T(8,128)(2,1)S(1)}, bf16[128,768]{1,0:T(8,128)(2,1)S(1)}, u32[]{:S(2)}, u32[]{:S(2)}) %collective-permute-start.36) | collective-permute-done | bytes 196640 | tf_op jit(solution)/shard_map/ppermute | solution.py:18
  307.0 6.0 %collective-permute-start.48 = (bf16[384,768]{1,0:T(8,128)(2,1)S(1)}, bf16[384,768]{1,0:T(8,128)(2,1)S(1)}, u32[]{:S(2)}, u32[]{:S(2)}) collective-permute-start(bf16[384,768]{1,0:T(8,128)(2,1)S(1)} %pad_maximum_fusion.16), channel_id=1, source_target_pairs={{0,1},{3,2},{4,5},{7,6},{8,9},{11,10},{12,13},{15,14},{16,17},{19,... | collective-permute-start | bytes 1769480 | tf_op jit(solution)/shard_map/ppermute | solution.py:350
  314.4 11.0 %collective-permute-done.48 = bf16[384,768]{1,0:T(8,128)(2,1)S(1)} collective-permute-done((bf16[384,768]{1,0:T(8,128)(2,1)S(1)}, bf16[384,768]{1,0:T(8,128)(2,1)S(1)}, u32[]{:S(2)}, u32[]{:S(2)}) %collective-permute-start.48) | collective-permute-done | bytes 589856 | tf_op jit(solution)/shard_map/ppermute | solution.py:350
  329.1 7.9 %collective-permute-start.53 = (bf16[387,768]{1,0:T(8,128)(2,1)S(1)}, bf16[387,768]{1,0:T(8,128)(2,1)S(1)}, u32[]{:S(2)}, u32[]{:S(2)}) collective-permute-start(bf16[387,768]{1,0:T(8,128)(2,1)S(1)} %pad_maximum_fusion.10), channel_id=1, source_target_pairs={{0,1},{3,2},{4,5},{7,6},{8,9},{11,10},{12,13},{15,14},{16,17},{19,... | collective-permute-start | bytes 1783304 | tf_op jit(solution)/shard_map/ppermute | solution.py:350
  340.0 10.1 %collective-permute-done.53 = bf16[387,768]{1,0:T(8,128)(2,1)S(1)} collective-permute-done((bf16[387,768]{1,0:T(8,128)(2,1)S(1)}, bf16[387,768]{1,0:T(8,128)(2,1)S(1)}, u32[]{:S(2)}, u32[]{:S(2)}) %collective-permute-start.53) | collective-permute-done | bytes 594464 | tf_op jit(solution)/shard_map/ppermute | solution.py:350
  351.0 10.6 %collective-permute-done.56 = bf16[768,768]{1,0:T(8,128)(2,1)S(1)} collective-permute-done((bf16[768,768]{1,0:T(8,128)(2,1)S(1)}, bf16[768,768]{1,0:T(8,128)(2,1)S(1)}, u32[]{:S(2)}, u32[]{:S(2)}) %collective-permute-start.56) | collective-permute-done | bytes 1179680 | tf_op jit(solution)/shard_map/ppermute | solution.py:350
  365.3 8.9 %collective-permute-done.58 = bf16[384,768]{1,0:T(8,128)(2,1)S(1)} collective-permute-done((bf16[384,768]{1,0:T(8,128)(2,1)S(1)}, bf16[384,768]{1,0:T(8,128)(2,1)S(1)}, u32[]{:S(2)}, u32[]{:S(2)}) %collective-permute-start.58) | collective-permute-done | bytes 589856 | tf_op jit(solution)/shard_map/ppermute | solution.py:350
  374.5 12.2 %collective-permute-done.57 = bf16[387,768]{1,0:T(8,128)(2,1)S(1)} collective-permute-done((bf16[387,768]{1,0:T(8,128)(2,1)S(1)}, bf16[387,768]{1,0:T(8,128)(2,1)S(1)}, u32[]{:S(2)}, u32[]{:S(2)}) %collective-permute-start.57) | collective-permute-done | bytes 594464 | tf_op jit(solution)/shard_map/ppermute | solution.py:350
  (512 shorter events, 138.7 us)
Async XLA Ops:
  8.5 28.4 %collective-permute-start = (bf16[128,768]{1,0:T(8,128)(2,1)}, bf16[128,768]{1,0:T(8,128)(2,1)}, u32[]{:S(2)}, u32[]{:S(2)}) collective-permute-start(bf16[128,768]{1,0:T(8,128)(2,1)} %dynamic-slice_bitcast_fusion.5), channel_id=1, source_target_pairs={{0,8},{4,12},{8,0},{12,4},{1,9},{5,13},{9,1},{13,5},{2,10},{6,14},... | collective-permute-start | bytes 589832 | tf_op jit(solution)/shard_map/ppermute | solution.py:18
  11.0 35.8 %collective-permute-start.5 = (bf16[192,2304]{1,0:T(8,128)(2,1)}, bf16[192,2304]{1,0:T(8,128)(2,1)}, u32[]{:S(2)}, u32[]{:S(2)}) collective-permute-start(bf16[192,2304]{1,0:T(8,128)(2,1)} %bitcast.190), channel_id=1, source_target_pairs={{0,8},{4,12},{8,0},{12,4},{1,9},{5,13},{9,1},{13,5},{2,10},{6,14},... | collective-permute-start | bytes 2654216 | tf_op jit(solution)/shard_map/ppermute | solution.py:18
  14.0 27.7 %collective-permute-start.4 = (bf16[192,1152]{1,0:T(8,128)(2,1)}, bf16[192,1152]{1,0:T(8,128)(2,1)}, u32[]{:S(2)}, u32[]{:S(2)}) collective-permute-start(bf16[192,1152]{1,0:T(8,128)(2,1)} %pad_maximum_fusion.18), channel_id=1, source_target_pairs={{0,4},{4,0},{8,12},{12,8},{1,5},{5,1},{9,13},{13,9},{2,6},{6,2},{1... | collective-permute-start | bytes 1327112 | tf_op jit(solution)/shard_map/ppermute | solution.py:22
  15.2 24.6 %collective-permute-start.13 = (bf16[192,768]{1,0:T(8,128)(2,1)}, bf16[192,768]{1,0:T(8,128)(2,1)S(1)}, u32[]{:S(2)}, u32[]{:S(2)}) collective-permute-start(bf16[192,768]{1,0:T(8,128)(2,1)} %get-tuple-element.150), channel_id=1, source_target_pairs={{0,4},{4,0},{8,12},{12,8},{1,5},{5,1},{9,13},{13,9},{2,6},{6,2},{1... | collective-permute-start | bytes 884744 | tf_op jit(solution)/shard_map/ppermute | solution.py:22
  17.8 18.1 %collective-permute-start.3 = (bf16[2,2304]{1,0:T(2,128)(2,1)S(1)}, bf16[2,2304]{1,0:T(2,128)(2,1)S(1)}, u32[]{:S(2)}, u32[]{:S(2)}) collective-permute-start(bf16[2,2304]{1,0:T(2,128)(2,1)S(1)} %pad_maximum_fusion.24), channel_id=1, source_target_pairs={{0,8},{4,12},{8,0},{12,4},{1,9},{5,13},{9,1},{13,5},{2,10},{6,14},... | collective-permute-start | bytes 27656 | tf_op jit(solution)/shard_map/ppermute | solution.py:18
  39.8 19.7 %collective-permute-start.11 = (bf16[192,1536]{1,0:T(8,128)(2,1)}, bf16[192,1536]{1,0:T(8,128)(2,1)S(1)}, u32[]{:S(2)}, u32[]{:S(2)}) collective-permute-start(bf16[192,1536]{1,0:T(8,128)(2,1)} %get-tuple-element.65), channel_id=1, source_target_pairs={{0,8},{4,12},{8,0},{12,4},{1,9},{5,13},{9,1},{13,5},{2,10},{6,14},... | collective-permute-start | bytes 1769480 | tf_op jit(solution)/shard_map/ppermute | solution.py:18
  46.9 14.5 %collective-permute-start.8 = (bf16[192,768]{1,0:T(8,128)(2,1)S(1)}, bf16[192,768]{1,0:T(8,128)(2,1)S(1)}, u32[]{:S(2)}, u32[]{:S(2)}) collective-permute-start(bf16[192,768]{1,0:T(8,128)(2,1)S(1)} %broadcast_select_fusion.14), channel_id=1, source_target_pairs={{0,4},{4,0},{8,12},{12,8},{1,5},{5,1},{9,13},{13,9},{2,6},{6,2},{1... | collective-permute-start | bytes 884744 | tf_op jit(solution)/shard_map/ppermute | solution.py:22
  48.4 13.3 %collective-permute-start.6 = (bf16[192,1152]{1,0:T(8,128)(2,1)S(1)}, bf16[192,1152]{1,0:T(8,128)(2,1)S(1)}, u32[]{:S(2)}, u32[]{:S(2)}) collective-permute-start(bf16[192,1152]{1,0:T(8,128)(2,1)S(1)} %pad_maximum_fusion.20), channel_id=1, source_target_pairs={{0,4},{4,0},{8,12},{12,8},{1,5},{5,1},{9,13},{13,9},{2,6},{6,2},{1... | collective-permute-start | bytes 1327112 | tf_op jit(solution)/shard_map/ppermute | solution.py:22
  48.9 23.2 %collective-permute-start.14 = (bf16[192,1536]{1,0:T(8,128)(2,1)S(1)}, bf16[192,1536]{1,0:T(8,128)(2,1)S(1)}, u32[]{:S(2)}, u32[]{:S(2)}) collective-permute-start(bf16[192,1536]{1,0:T(8,128)(2,1)S(1)} %copy-done.78), channel_id=1, source_target_pairs={{0,8},{4,12},{8,0},{12,4},{1,9},{5,13},{9,1},{13,5},{2,10},{6,14},... | collective-permute-start | bytes 1769480 | tf_op jit(solution)/shard_map/ppermute | solution.py:18
  59.5 37.6 %collective-permute-start.12 = (bf16[192,768]{1,0:T(8,128)(2,1)S(1)}, bf16[192,768]{1,0:T(8,128)(2,1)S(1)}, u32[]{:S(2)}, u32[]{:S(2)}) collective-permute-start(bf16[192,768]{1,0:T(8,128)(2,1)S(1)} %constant_dynamic-slice_fusion.20), channel_id=1, source_target_pairs={{0,4},{4,0},{8,12},{12,8},{1,5},{5,1},{9,13},{13,9},{2,6},{6,2},{1... | collective-permute-start | bytes 884744 | tf_op jit(solution)/shard_map/ppermute | solution.py:22
  59.6 25.2 %collective-permute-start.16 = (bf16[384,768]{1,0:T(8,128)(2,1)S(1)}, bf16[384,768]{1,0:T(8,128)(2,1)S(1)}, u32[]{:S(2)}, u32[]{:S(2)}) collective-permute-start(bf16[384,768]{1,0:T(8,128)(2,1)S(1)} %copy-done.77), channel_id=1, source_target_pairs={{0,8},{4,12},{8,0},{12,4},{1,9},{5,13},{9,1},{13,5},{2,10},{6,14},... | collective-permute-start | bytes 1769480 | tf_op jit(solution)/shard_map/ppermute | solution.py:18
  61.4 35.6 %collective-permute-start.17 = (bf16[384,768]{1,0:T(8,128)(2,1)S(1)}, bf16[384,768]{1,0:T(8,128)(2,1)S(1)}, u32[]{:S(2)}, u32[]{:S(2)}) collective-permute-start(bf16[384,768]{1,0:T(8,128)(2,1)S(1)} %copy-done.76), channel_id=1, source_target_pairs={{0,8},{4,12},{8,0},{12,4},{1,9},{5,13},{9,1},{13,5},{2,10},{6,14},... | collective-permute-start | bytes 1769480 | tf_op jit(solution)/shard_map/ppermute | solution.py:18
  72.1 25.0 %collective-permute-start.15 = (bf16[192,768]{1,0:T(8,128)(2,1)S(1)}, bf16[192,768]{1,0:T(8,128)(2,1)S(1)}, u32[]{:S(2)}, u32[]{:S(2)}) collective-permute-start(bf16[192,768]{1,0:T(8,128)(2,1)S(1)} %constant_dynamic-slice_fusion.18), channel_id=1, source_target_pairs={{0,4},{4,0},{8,12},{12,8},{1,5},{5,1},{9,13},{13,9},{2,6},{6,2},{1... | collective-permute-start | bytes 884744 | tf_op jit(solution)/shard_map/ppermute | solution.py:22
  82.0 15.8 %collective-permute-start.9 = (bf16[512,768]{1,0:T(8,128)(2,1)S(1)}, bf16[512,768]{1,0:T(8,128)(2,1)S(1)}, u32[]{:S(2)}, u32[]{:S(2)}) collective-permute-start(bf16[512,768]{1,0:T(8,128)(2,1)S(1)} %get-tuple-element.64), channel_id=1, source_target_pairs={{0,4},{4,0},{8,12},{12,8},{1,5},{5,1},{9,13},{13,9},{2,6},{6,2},{1... | collective-permute-start | bytes 2359304 | tf_op jit(solution)/shard_map/ppermute | solution.py:22
  166.3 13.7 %collective-permute-start.29 = (bf16[256,768]{1,0:T(8,128)(2,1)}, bf16[256,768]{1,0:T(8,128)(2,1)}, u32[]{:S(2)}, u32[]{:S(2)}) collective-permute-start(bf16[256,768]{1,0:T(8,128)(2,1)} %fusion.37), channel_id=1, source_target_pairs={{16,0},{17,1},{18,2},{19,3},{20,4},{21,5},{22,6},{23,7},{24,8},{25... | collective-permute-start | bytes 1179656 | tf_op jit(solution)/shard_map/ppermute | solution.py:475
  188.3 32.6 %collective-permute-start.33 = (bf16[768,768]{1,0:T(8,128)(2,1)}, bf16[768,768]{1,0:T(8,128)(2,1)}, u32[]{:S(2)}, u32[]{:S(2)}) collective-permute-start(bf16[768,768]{1,0:T(8,128)(2,1)} %convolution_convert_fusion.1), channel_id=1, source_target_pairs={{0,8},{4,12},{8,0},{12,4},{1,9},{5,13},{9,1},{13,5},{2,10},{6,14},... | collective-permute-start | bytes 3538952 | tf_op jit(solution)/shard_map/ppermute | solution.py:18
  195.8 59.0 %collective-permute-start.40 = (bf16[384,768]{1,0:T(8,128)(2,1)}, bf16[384,768]{1,0:T(8,128)(2,1)}, u32[]{:S(2)}, u32[]{:S(2)}) collective-permute-start(bf16[384,768]{1,0:T(8,128)(2,1)} %convolution_convert_fusion.3), channel_id=1, source_target_pairs={{0,8},{4,12},{8,0},{12,4},{1,9},{5,13},{9,1},{13,5},{2,10},{6,14},... | collective-permute-start | bytes 1769480 | tf_op jit(solution)/shard_map/ppermute | solution.py:18
  199.1 53.8 %collective-permute-start.41 = (bf16[384,768]{1,0:T(8,128)(2,1)}, bf16[384,768]{1,0:T(8,128)(2,1)}, u32[]{:S(2)}, u32[]{:S(2)}) collective-permute-start(bf16[384,768]{1,0:T(8,128)(2,1)} %convolution_convert_fusion.2), channel_id=1, source_target_pairs={{0,8},{4,12},{8,0},{12,4},{1,9},{5,13},{9,1},{13,5},{2,10},{6,14},... | collective-permute-start | bytes 1769480 | tf_op jit(solution)/shard_map/ppermute | solution.py:18
  224.0 28.9 %collective-permute-start.38 = (bf16[768,768]{1,0:T(8,128)(2,1)}, bf16[768,768]{1,0:T(8,128)(2,1)}, u32[]{:S(2)}, u32[]{:S(2)}) collective-permute-start(bf16[768,768]{1,0:T(8,128)(2,1)} %add_convert_fusion.4), channel_id=1, source_target_pairs={{0,1},{3,2},{4,5},{7,6},{8,9},{11,10},{12,13},{15,14},{16,17},{19,... | collective-permute-start | bytes 3538952 | tf_op jit(solution)/shard_map/ppermute | solution.py:350
  230.5 65.1 %collective-permute-start.43 = (bf16[384,768]{1,0:T(8,128)(2,1)}, bf16[384,768]{1,0:T(8,128)(2,1)}, u32[]{:S(2)}, u32[]{:S(2)}) collective-permute-start(bf16[384,768]{1,0:T(8,128)(2,1)} %slice.239), channel_id=1, source_target_pairs={{0,8},{4,12},{8,0},{12,4},{1,9},{5,13},{9,1},{13,5},{2,10},{6,14},... | collective-permute-start | bytes 1769480 | tf_op jit(solution)/shard_map/ppermute | solution.py:18
  233.3 92.1 %collective-permute-start.37 = (bf16[384,768]{1,0:T(8,128)(2,1)}, bf16[384,768]{1,0:T(8,128)(2,1)}, u32[]{:S(2)}, u32[]{:S(2)}) collective-permute-start(bf16[384,768]{1,0:T(8,128)(2,1)} %maximum_maximum_fusion), channel_id=1, source_target_pairs={{0,8},{4,12},{8,0},{12,4},{1,9},{5,13},{9,1},{13,5},{2,10},{6,14},... | collective-permute-start | bytes 1769480 | tf_op jit(solution)/shard_map/ppermute | solution.py:18
  263.2 32.3 %collective-permute-start.46 = (bf16[768,768]{1,0:T(8,128)(2,1)}, bf16[768,768]{1,0:T(8,128)(2,1)}, u32[]{:S(2)}, u32[]{:S(2)}) collective-permute-start(bf16[768,768]{1,0:T(8,128)(2,1)} %pad_maximum_fusion.3), channel_id=1, source_target_pairs={{0,1},{3,2},{4,5},{7,6},{8,9},{11,10},{12,13},{15,14},{16,17},{19,... | collective-permute-start | bytes 3538952 | tf_op jit(solution)/shard_map/ppermute | solution.py:350
  272.7 26.7 %collective-permute-start.35 = (bf16[128,768]{1,0:T(8,128)(2,1)S(1)}, bf16[128,768]{1,0:T(8,128)(2,1)S(1)}, u32[]{:S(2)}, u32[]{:S(2)}) collective-permute-start(bf16[128,768]{1,0:T(8,128)(2,1)S(1)} %constant_dynamic-slice_fusion.12), channel_id=1, source_target_pairs={{0,4},{4,0},{8,12},{12,8},{1,5},{5,1},{9,13},{13,9},{2,6},{6,2},{1... | collective-permute-start | bytes 589832 | tf_op jit(solution)/shard_map/ppermute | solution.py:22
  275.1 50.3 %collective-permute-start.42 = (bf16[768,768]{1,0:T(8,128)(2,1)S(1)}, bf16[768,768]{1,0:T(8,128)(2,1)S(1)}, u32[]{:S(2)}, u32[]{:S(2)}) collective-permute-start(bf16[768,768]{1,0:T(8,128)(2,1)S(1)} %add_convert_fusion.2), channel_id=1, source_target_pairs={{1,0},{2,3},{5,4},{6,7},{9,8},{10,11},{13,12},{14,15},{17,16},{18,... | collective-permute-start | bytes 3538952 | tf_op jit(solution)/shard_map/ppermute | solution.py:350
  297.2 16.9 %collective-permute-start.49 = (bf16[768,768]{1,0:T(8,128)(2,1)S(1)}, bf16[768,768]{1,0:T(8,128)(2,1)S(1)}, u32[]{:S(2)}, u32[]{:S(2)}) collective-permute-start(bf16[768,768]{1,0:T(8,128)(2,1)S(1)} %add_convert_fusion.1), channel_id=1, source_target_pairs={{1,2},{2,1},{5,6},{6,5},{9,10},{10,9},{13,14},{14,13},{17,18},{18,... | collective-permute-start | bytes 3538952 | tf_op jit(solution)/shard_map/ppermute | solution.py:350
  301.0 24.4 %collective-permute-start.52 = (bf16[3,768]{1,0:T(4,128)(2,1)S(1)}, bf16[3,768]{1,0:T(4,128)(2,1)S(1)}, u32[]{:S(2)}, u32[]{:S(2)}) collective-permute-start(bf16[3,768]{1,0:T(4,128)(2,1)S(1)} %fusion.91), channel_id=1, source_target_pairs={{0,8},{4,12},{8,0},{12,4},{1,9},{5,13},{9,1},{13,5},{2,10},{6,14},... | collective-permute-start | bytes 13832 | tf_op jit(solution)/shard_map/ppermute | solution.py:18
  307.0 18.4 %collective-permute-start.48 = (bf16[384,768]{1,0:T(8,128)(2,1)S(1)}, bf16[384,768]{1,0:T(8,128)(2,1)S(1)}, u32[]{:S(2)}, u32[]{:S(2)}) collective-permute-start(bf16[384,768]{1,0:T(8,128)(2,1)S(1)} %pad_maximum_fusion.16), channel_id=1, source_target_pairs={{0,1},{3,2},{4,5},{7,6},{8,9},{11,10},{12,13},{15,14},{16,17},{19,... | collective-permute-start | bytes 1769480 | tf_op jit(solution)/shard_map/ppermute | solution.py:350
  327.7 33.9 %collective-permute-start.56 = (bf16[768,768]{1,0:T(8,128)(2,1)S(1)}, bf16[768,768]{1,0:T(8,128)(2,1)S(1)}, u32[]{:S(2)}, u32[]{:S(2)}) collective-permute-start(bf16[768,768]{1,0:T(8,128)(2,1)S(1)} %add_convert_fusion), channel_id=1, source_target_pairs={{1,0},{2,3},{5,4},{6,7},{9,8},{10,11},{13,12},{14,15},{17,16},{18,... | collective-permute-start | bytes 3538952 | tf_op jit(solution)/shard_map/ppermute | solution.py:350
  329.1 21.1 %collective-permute-start.53 = (bf16[387,768]{1,0:T(8,128)(2,1)S(1)}, bf16[387,768]{1,0:T(8,128)(2,1)S(1)}, u32[]{:S(2)}, u32[]{:S(2)}) collective-permute-start(bf16[387,768]{1,0:T(8,128)(2,1)S(1)} %pad_maximum_fusion.10), channel_id=1, source_target_pairs={{0,1},{3,2},{4,5},{7,6},{8,9},{11,10},{12,13},{15,14},{16,17},{19,... | collective-permute-start | bytes 1783304 | tf_op jit(solution)/shard_map/ppermute | solution.py:350
  338.7 35.5 %collective-permute-start.58 = (bf16[384,768]{1,0:T(8,128)(2,1)S(1)}, bf16[384,768]{1,0:T(8,128)(2,1)S(1)}, u32[]{:S(2)}, u32[]{:S(2)}) collective-permute-start(bf16[384,768]{1,0:T(8,128)(2,1)S(1)} %add_convert_fusion.10), channel_id=1, source_target_pairs={{1,0},{2,3},{5,4},{6,7},{9,8},{10,11},{13,12},{14,15},{17,16},{18,... | collective-permute-start | bytes 1769480 | tf_op jit(solution)/shard_map/ppermute | solution.py:350
  350.3 13.5 %collective-permute-start.55 = (bf16[387,768]{1,0:T(8,128)(2,1)S(1)}, bf16[387,768]{1,0:T(8,128)(2,1)S(1)}, u32[]{:S(2)}, u32[]{:S(2)}) collective-permute-start(bf16[387,768]{1,0:T(8,128)(2,1)S(1)} %add_convert_fusion.9), channel_id=1, source_target_pairs={{1,2},{2,1},{5,6},{6,5},{9,10},{10,9},{13,14},{14,13},{17,18},{18,... | collective-permute-start | bytes 1783304 | tf_op jit(solution)/shard_map/ppermute | solution.py:350
  364.0 22.7 %collective-permute-start.57 = (bf16[387,768]{1,0:T(8,128)(2,1)S(1)}, bf16[387,768]{1,0:T(8,128)(2,1)S(1)}, u32[]{:S(2)}, u32[]{:S(2)}) collective-permute-start(bf16[387,768]{1,0:T(8,128)(2,1)S(1)} %add_convert_fusion.8), channel_id=1, source_target_pairs={{1,0},{2,3},{5,4},{6,7},{9,8},{10,11},{13,12},{14,15},{17,16},{18,... | collective-permute-start | bytes 1783304 | tf_op jit(solution)/shard_map/ppermute | solution.py:350
  (133 other events, 1347.7 us)
